TPU v7x, 32 devices: a whole 2x2x4 slice. The times are simulated.
32 devices in a mesh: dp: 16 (over z, x, core), band: 2 (over y).
Axes of the slice: x: 2, y: 2, z: 4, core: 2. Of those that a mesh axis runs over, the one named last changes fastest.
Arguments:
- block_input: bfloat16 [16, 5, 32, 16, 1024], P('dp', None, 'band'), may hold values from -6 to 6
- modulation: float32 [16, 6, 1024], P('dp'), may hold values from -2 to 2
- band_live: int32 [16, 2], P('dp'), may hold values 0 or 1
- w_query: bfloat16 [1024, 1024], replicated, may hold values from -0.25 to 0.25
- w_key: bfloat16 [1024, 1024], replicated, may hold values from -0.25 to 0.25
- w_value: bfloat16 [1024, 1024], replicated, may hold values from -0.1875 to 0.1875
- w_out: bfloat16 [1024, 1024], replicated, may hold values from -0.5 to 0.5
- w_up: bfloat16 [1024, 4096], replicated, may hold values from -0.1875 to 0.1875
- w_down: bfloat16 [4096, 1024], replicated, may hold values from -0.09375 to 0.09375
- cotangent: bfloat16 [16, 5, 32, 16, 1024], P('dp', None, 'band'), may hold values from -6 to 6
Outputs:
- block_output: bfloat16 [16, 5, 32, 16, 1024], P('dp', None, 'band')
- grad_input: bfloat16 [16, 5, 32, 16, 1024], P('dp', None, 'band')
- grad_modulation: float32 [16, 6, 1024], P('dp')
- grad_w_query: float32 [1048576], P('dp')
- grad_w_key: float32 [1048576], P('dp')
- grad_w_value: float32 [1048576], P('dp')
- grad_w_out: float32 [1048576], P('dp')
- grad_w_up: float32 [4194304], P('dp')
- grad_w_down: float32 [4194304], P('dp')
Inputs may be any that keep to these rules, and one draw needn't show every extreme that they name: band_live[c, b] is 1 where band b of clip c holds latent rows and 0 where that band slot is empty; an empty band's tokens pass the block unchanged.
All inputs are finite; a program needn't handle non-finite values.
Results may differ from a plain program's by a relative error of at most 0.015.
The roundings to bfloat16 on the way count: a program that leaves them out, or rounds other values in their place, can miss the bound.
Values may be sent and summed in bfloat16 or wider, within the bound.
A program may use at most 384 MiB of HBM per device.

v0:
```python
import jax
import jax.numpy as jnp
from jax import lax
from jax.sharding import PartitionSpec as P

HEADS = 16
HEAD_DIM = 64


epsilon = 1e-06
masked_score = -1e30


def padded(cells, sides, width):
    for axis, dim in sides:
        count = lax.axis_size(axis)
        ends = count - 1
        head = lax.slice_in_dim(cells, 0, width, axis=dim)
        tail = lax.slice_in_dim(cells, cells.shape[dim] - width, cells.shape[dim], axis=dim)
        cells = jnp.concatenate(
            [
                lax.ppermute(tail, axis, [(i, (i + 1) % count) for i in range(ends)]),
                cells,
                lax.ppermute(head, axis, [((i + 1) % count, i) for i in range(ends)]),
            ],
            axis=dim,
        )
    return cells


def passed_along(block, axis, distance):
    devices = range(lax.axis_size(axis))
    route = [(i - distance, i) for i in devices if i - distance in devices]
    return lax.ppermute(block, axis, route)


def layer_norm(values):
    centred = values - jnp.mean(values, axis=-1, keepdims=True)
    spread = jnp.mean(centred * centred, axis=-1, keepdims=True)
    return centred * lax.rsqrt(spread + epsilon)


def modulate(values, scale_row, shift_row):
    return layer_norm(values) * (1.0 + scale_row) + shift_row


def matmul(left, right):
    return jnp.dot(left, right, preferred_element_type=jnp.float32)


def outer_sum(left, right):
    return lax.dot_general(
        left, right, (((0,), (0,)), ((), ())), preferred_element_type=jnp.float32
    )


def back_product(left, right):
    return lax.dot_general(
        left, right, (((1,), (1,)), ((), ())), preferred_element_type=jnp.float32
    )


def to_windows(field_in):
    frame_count, row_count, col_count, model_width = field_in.shape
    blocks = field_in.reshape(frame_count, row_count // 8, 8, col_count // 8, 8, model_width)
    blocks = blocks.transpose(1, 3, 0, 2, 4, 5)
    return blocks.reshape(row_count // 8 * (col_count // 8), frame_count * 64, model_width)


def from_windows(windows, frame_count, row_count, col_count):
    model_width = windows.shape[-1]
    blocks = windows.reshape(row_count // 8, col_count // 8, frame_count, 8, 8, model_width)
    blocks = blocks.transpose(2, 0, 3, 1, 4, 5)
    return blocks.reshape(frame_count, row_count, col_count, model_width)


def windowed(field_in):
    windows = to_windows(field_in)
    return windows.reshape(windows.shape[0], windows.shape[1], HEADS, HEAD_DIM)


def on_device(
    block_input, modulation, band_live, w_query, w_key, w_value, w_out, w_up, w_down, cotangent
):
    frames, rows_own, col_count, model_width = block_input.shape[1:]
    token_count = frames * rows_own * col_count
    field_shape = (frames, rows_own, col_count, model_width)
    padding = ((0, 0), (4, 4), (0, 0), (0, 0))
    score_scale = HEAD_DIM ** (-0.5)
    band_count = lax.axis_size("band")
    band_index = lax.axis_index("band")
    band_flags = band_live[0]
    positions = jnp.arange(band_count, dtype=jnp.int32)

    def band_state(offset):
        return jnp.sum(jnp.where(positions == band_index + offset, band_flags, 0)) == 1

    live_own = band_state(0)
    live_prev = band_state(-1)
    live_next = band_state(1)
    has_prev = band_index > 0
    has_next = band_index < band_count - 1
    gate_live = live_own.astype(jnp.float32)
    mod_rows = modulation[0]
    inputs = block_input[0].reshape(token_count, model_width).astype(jnp.float32)
    normed_low = modulate(inputs, mod_rows[1], mod_rows[0]).astype(jnp.bfloat16)
    queries = matmul(normed_low, w_query).astype(jnp.bfloat16)
    key_rows = matmul(normed_low, w_key).astype(jnp.bfloat16)
    value_rows = matmul(normed_low, w_value).astype(jnp.bfloat16)
    stacked = jnp.stack([key_rows.reshape(field_shape), value_rows.reshape(field_shape)])
    extended = padded(stacked, (("band", 2),), 4)
    keys_pad = extended[0]
    values_pad = extended[1]
    queries_pad = jnp.pad(queries.reshape(field_shape), padding)
    win_query = windowed(queries_pad)
    win_key = windowed(keys_pad)
    win_value = windowed(values_pad)
    top_ok = has_prev & (live_prev | jnp.logical_not(live_own))
    bottom_ok = has_next & (live_next | jnp.logical_not(live_own))
    row_flags = jnp.concatenate(
        [jnp.full((4,), top_ok), jnp.ones((rows_own,), jnp.bool_), jnp.full((4,), bottom_ok)]
    )
    flag_field = jnp.broadcast_to(
        row_flags[None, :, None, None], (frames, rows_own + 8, col_count, 1)
    )
    key_ok = to_windows(flag_field)[:, :, 0]

    def score_block(query_win, key_win):
        raw = (
            jnp.einsum("wqhd,wkhd->whqk", query_win, key_win, preferred_element_type=jnp.float32)
            * score_scale
        )
        return jnp.where(key_ok[:, None, None, :], raw, masked_score)

    scores = score_block(win_query, win_key)
    row_top = jnp.max(scores, axis=-1, keepdims=True)
    log_total = row_top + jnp.log(jnp.sum(jnp.exp(scores - row_top), axis=-1, keepdims=True))
    attn_low = jnp.exp(scores - log_total).astype(jnp.bfloat16)
    blended = jnp.einsum("whqk,wkhd->wqhd", attn_low, win_value, preferred_element_type=jnp.float32)
    blended = blended.reshape(blended.shape[0], blended.shape[1], model_width)
    attended = from_windows(blended, frames, rows_own + 8, col_count)[:, 4 : 4 + rows_own]
    attended = attended.reshape(token_count, model_width).astype(jnp.bfloat16)
    attn_out = matmul(attended, w_out)
    middle = inputs + gate_live * mod_rows[2] * attn_out
    normed_mid = modulate(middle, mod_rows[4], mod_rows[3]).astype(jnp.bfloat16)
    pre_act = matmul(normed_mid, w_up)
    hidden_low = jax.nn.gelu(pre_act).astype(jnp.bfloat16)
    mlp_out = matmul(hidden_low, w_down)
    result = middle + gate_live * mod_rows[5] * mlp_out
    block_output = result.astype(jnp.bfloat16).reshape(block_input.shape)
    grad_out = cotangent[0].reshape(token_count, model_width).astype(jnp.float32)
    grad_mlp = (gate_live * mod_rows[5] * grad_out).astype(jnp.bfloat16)
    gate_m_grad = jnp.sum(gate_live * mlp_out * grad_out, axis=0)
    down_grad = outer_sum(hidden_low, grad_mlp)
    grad_hidden = back_product(grad_mlp, w_down)
    gelu_value, gelu_pull = jax.vjp(jax.nn.gelu, pre_act)
    grad_pre = gelu_pull(grad_hidden)[0].astype(jnp.bfloat16)
    up_grad = outer_sum(normed_mid, grad_pre)
    grad_normed_mid = back_product(grad_pre, w_up)
    mid_value, mid_pull = jax.vjp(modulate, middle, mod_rows[4], mod_rows[3])
    grad_mid_norm, scale_m_grad, shift_m_grad = mid_pull(grad_normed_mid)
    grad_middle = grad_out + grad_mid_norm
    grad_attn = (gate_live * mod_rows[2] * grad_middle).astype(jnp.bfloat16)
    gate_a_grad = jnp.sum(gate_live * attn_out * grad_middle, axis=0)
    out_grad = outer_sum(attended, grad_attn)
    grad_attended = back_product(grad_attn, w_out).astype(jnp.bfloat16)
    win_grad_out = windowed(jnp.pad(grad_attended.reshape(field_shape), padding))
    scores_again = score_block(win_query, win_key)
    probs = jnp.exp(scores_again - log_total)
    probs_low = probs.astype(jnp.bfloat16)
    grad_probs = jnp.einsum(
        "wqhd,wkhd->whqk", win_grad_out, win_value, preferred_element_type=jnp.float32
    )
    row_dot = jnp.sum(probs * grad_probs, axis=-1, keepdims=True)
    grad_scores = (probs * (grad_probs - row_dot)).astype(jnp.bfloat16)
    win_grad_query = (
        jnp.einsum("whqk,wkhd->wqhd", grad_scores, win_key, preferred_element_type=jnp.float32)
        * score_scale
    )
    win_grad_key = (
        jnp.einsum("whqk,wqhd->wkhd", grad_scores, win_query, preferred_element_type=jnp.float32)
        * score_scale
    )
    win_grad_value = jnp.einsum(
        "whqk,wqhd->wkhd", probs_low, win_grad_out, preferred_element_type=jnp.float32
    )
    win_rows = win_grad_query.shape[1]

    def unwindow(windows):
        return from_windows(
            windows.reshape(windows.shape[0], win_rows, model_width),
            frames,
            rows_own + 8,
            col_count,
        )

    grad_queries = (
        unwindow(win_grad_query)[:, 4 : 4 + rows_own]
        .reshape(token_count, model_width)
        .astype(jnp.bfloat16)
    )
    grad_pairs = jnp.stack([unwindow(win_grad_key), unwindow(win_grad_value)])
    from_next = passed_along(grad_pairs[:, :, :4].astype(jnp.bfloat16), "band", -1).astype(
        jnp.float32
    )
    from_prev = passed_along(
        grad_pairs[:, :, 4 + rows_own :].astype(jnp.bfloat16), "band", 1
    ).astype(jnp.float32)
    own_pairs = grad_pairs[:, :, 4 : 4 + rows_own]
    own_pairs = own_pairs + jnp.pad(from_prev, ((0, 0), (0, 0), (0, rows_own - 4), (0, 0), (0, 0)))
    own_pairs = own_pairs + jnp.pad(from_next, ((0, 0), (0, 0), (rows_own - 4, 0), (0, 0), (0, 0)))
    grad_keys = own_pairs[0].reshape(token_count, model_width).astype(jnp.bfloat16)
    grad_values = own_pairs[1].reshape(token_count, model_width).astype(jnp.bfloat16)
    query_grad = outer_sum(normed_low, grad_queries)
    key_grad = outer_sum(normed_low, grad_keys)
    value_grad = outer_sum(normed_low, grad_values)
    grad_normed = (
        back_product(grad_queries, w_query)
        + back_product(grad_keys, w_key)
        + back_product(grad_values, w_value)
    )
    in_value, in_pull = jax.vjp(modulate, inputs, mod_rows[1], mod_rows[0])
    grad_in_norm, scale_a_grad, shift_a_grad = in_pull(grad_normed)
    grad_input = (grad_middle + grad_in_norm).astype(jnp.bfloat16).reshape(block_input.shape)
    mod_partial = jnp.stack(
        [shift_a_grad, scale_a_grad, gate_a_grad, shift_m_grad, scale_m_grad, gate_m_grad]
    )
    shards = (
        lax.psum_scatter(query_grad.reshape(-1), "dp", scatter_dimension=0, tiled=True),
        lax.psum_scatter(key_grad.reshape(-1), "dp", scatter_dimension=0, tiled=True),
        lax.psum_scatter(value_grad.reshape(-1), "dp", scatter_dimension=0, tiled=True),
        lax.psum_scatter(out_grad.reshape(-1), "dp", scatter_dimension=0, tiled=True),
        lax.psum_scatter(up_grad.reshape(-1), "dp", scatter_dimension=0, tiled=True),
        lax.psum_scatter(down_grad.reshape(-1), "dp", scatter_dimension=0, tiled=True),
    )
    pieces = (
        lax.psum_scatter(
            shards[0].astype(jnp.bfloat16), "band", scatter_dimension=0, tiled=True
        ).astype(jnp.float32),
        lax.psum_scatter(
            shards[1].astype(jnp.bfloat16), "band", scatter_dimension=0, tiled=True
        ).astype(jnp.float32),
        lax.psum_scatter(
            shards[2].astype(jnp.bfloat16), "band", scatter_dimension=0, tiled=True
        ).astype(jnp.float32),
        lax.psum_scatter(
            shards[3].astype(jnp.bfloat16), "band", scatter_dimension=0, tiled=True
        ).astype(jnp.float32),
        lax.psum_scatter(
            shards[4].astype(jnp.bfloat16), "band", scatter_dimension=0, tiled=True
        ).astype(jnp.float32),
        lax.psum_scatter(
            shards[5].astype(jnp.bfloat16), "band", scatter_dimension=0, tiled=True
        ).astype(jnp.float32),
    )
    gradients = (
        lax.all_gather(pieces[0].astype(jnp.bfloat16), "band", axis=0, tiled=True).astype(
            jnp.float32
        ),
        lax.all_gather(pieces[1].astype(jnp.bfloat16), "band", axis=0, tiled=True).astype(
            jnp.float32
        ),
        lax.all_gather(pieces[2].astype(jnp.bfloat16), "band", axis=0, tiled=True).astype(
            jnp.float32
        ),
        lax.all_gather(pieces[3].astype(jnp.bfloat16), "band", axis=0, tiled=True).astype(
            jnp.float32
        ),
        lax.all_gather(pieces[4].astype(jnp.bfloat16), "band", axis=0, tiled=True).astype(
            jnp.float32
        ),
        lax.all_gather(pieces[5].astype(jnp.bfloat16), "band", axis=0, tiled=True).astype(
            jnp.float32
        ),
    )
    mod_total = lax.psum(mod_partial, "band")
    return (
        block_output,
        grad_input,
        mod_total[None],
        gradients[0],
        gradients[1],
        gradients[2],
        gradients[3],
        gradients[4],
        gradients[5],
    )


def solution(mesh):
    return jax.shard_map(
        on_device,
        mesh=mesh,
        in_specs=(
            P("dp", None, "band", None, None),
            P("dp", None, None),
            P("dp", None),
            P(),
            P(),
            P(),
            P(),
            P(),
            P(),
            P("dp", None, "band", None, None),
        ),
        out_specs=(
            P("dp", None, "band", None, None),
            P("dp", None, "band", None, None),
            P("dp", None, None),
            P("dp"),
            P("dp"),
            P("dp"),
            P("dp"),
            P("dp"),
            P("dp"),
        ),
        check_vma=False,
    )
```

profile of v0, /device:TPU:0, one launch (start us, length us, event | category | flops | bytes accessed | tf_op | source)
XLA Modules:
  0.0 1888.7 jit_solution(1585144567633088217)
XLA Ops:
  27.1 6.1 collective-permute-start
  35.6 14.3 fusion.65
  51.6 5.3 convolution_convert_fusion.1
  59.8 11.2 reshape_reshape.26
  71.0 11.3 copy.76
  97.9 11.2 reshape_reshape.25
  109.1 11.3 copy.78
  124.9 11.6 reshape_reshape.27
  136.5 11.2 copy.77
  147.7 23.7 %fusion = (f32[6,16,320]{2,1,0:T(8,128)S(1)}, f32[6,16,320,320]{2,3,1,0:T(8,128)}) fusion(pred[6,320]{1,0:T(8,128)(4,1)S(1)} %transpose.64, bf16[6,320,16,64]{1,3,2,0:T(8,128)(2,1)} %copy.76, bf16[6,320,16,64]{1,3,2,0:T(8,128)(2,1)} %copy.77), kind=kOutput, calls=%fused_computation.5 | convolution fusion | flops 1287751680 | bytes 47310720 | tf_op jit(solution)/shard_map/wqhd,wkhd->whqk/dot_general | solution.py:130
  171.4 20.5 %exponential_reduce_fusion = f32[6,16,320]{2,1,0:T(8,128)S(1)} fusion(f32[6,16,320,320]{2,3,1,0:T(8,128)} %get-tuple-element.57, f32[6,16,320]{2,1,0:T(8,128)S(1)} %get-tuple-element.56, pred[6,320]{1,0:T(8,128)(4,1)S(1)} %transpose.64), kind=kLoop, calls=%fused_computation.3 | loop fusion | flops 39290880 | bytes 39569280 | tf_op jit(solution)/shard_map/reduce_sum | solution.py:137
  191.9 23.3 %convert_bitcast_fusion = bf16[6,320,16,64]{1,3,2,0:T(8,128)(2,1)} fusion(bf16[6,320,16,64]{1,3,2,0:T(8,128)(2,1)} %copy.78, f32[6,16,320,320]{2,3,1,0:T(8,128)} %get-tuple-element.57, f32[6,16,320]{2,1,0:T(8,128)S(1)} %log_add_fusion, pred[6,320]{1,0:T(8,128)(4,1)S(1)} %transpose.64), kind=kOutput, calls=%fused_computation.67 | convolution fusion | flops 1299578880 | bytes 47310720 | tf_op jit(solution)/shard_map/whqk,wkhd->wqhd/dot_general | solution.py:139
  215.3 11.2 copy.80
  226.5 11.4 reshape_reshape.28
  240.8 6.0 fusion.61
  249.8 33.5 %fusion.8 = (bf16[1280,4096]{1,0:T(8,128)(2,1)}, f32[1280,4096]{1,0:T(8,128)}) fusion(f32[1280,4096]{1,0:T(8,128)} %fusion.65, bf16[1024,4096]{1,0:T(8,128)(2,1)} %param.17, f32[1280,1024]{1,0:T(8,128)} %copy-done.10, f32[1024]{0:T(1024)S(1)} %bitcast.248, f32[1024]{0:T(1024)S(1)} %bitcast.250, f32[1280]{0:T(1024)S(1)} %fusion.48, ...), kind=kOutput, calls=%fused_computation.15 | convolution fusion | flops 10848829440 | bytes 66078720 | tf_op jit(solution)/shard_map/dot_general | solution.py:48
  283.3 20.1 %multiply_reduce_fusion.1 = (f32[1024]{0:T(1024)}, f32[1280]{0:T(1024)S(1)}, f32[1024]{0:T(1024)}, f32[1280,1024]{1,0:T(8,128)}) fusion(f32[1280,1024]{1,0:T(8,128)} %copy-done.10, f32[1280]{0:T(1024)S(1)} %fusion.48, f32[1280]{0:T(1024)S(1)} %broadcast_multiply_fusion.1, f32[1024]{0:T(1024)S(1)} %bitcast.251, bf16[1280,4096]{1,0:T(8,128)(2,1)} %get-tuple-element.59, ...), kind=kOutput, calls=%fused_computation.58 | convolution fusion | flops 10747900928 | bytes 29387776 | tf_op jit(solution)/shard_map/dot_general | solution.py:58
  303.4 28.8 %fusion.14 = (f32[1024]{0:T(1024)}, bf16[1280,1024]{1,0:T(8,128)(2,1)}, f32[1280]{0:T(1024)S(1)}, f32[1280,1024]{1,0:T(8,128)}) fusion(bf16[1,5,16,16,1024]{4,3,2,1,0:T(8,128)(2,1)} %param.19, f32[]{:T(128)S(6)} %convert_element_type.158, f32[1280,1024]{1,0:T(8,128)} %copy-done.10, f32[1024]{0:T(1024)S(1)} %bitcast.240, ...), kind=kOutput, calls=%fused_computation.35 | convolution fusion | flops 10802952192 | bytes 50364420 | tf_op jit(solution)/shard_map/dot_general | solution.py:48
  332.2 6.5 multiply_reduce_fusion.2
  344.8 11.2 reshape_reshape.29
  356.0 11.3 copy.83
  367.3 36.1 %multiply_reduce_fusion = (f32[6,16,320]{2,1,0:T(8,128)S(1)}, f32[6,16,320,320]{2,3,1,0:T(8,128)}) fusion(f32[6,16,320,320]{2,3,1,0:T(8,128)} %get-tuple-element.57, f32[6,16,320]{2,1,0:T(8,128)S(1)} %log_add_fusion, pred[6,320]{1,0:T(8,128)(4,1)S(1)} %transpose.64, bf16[6,320,16,64]{1,3,2,0:T(8,128)(2,1)} %copy.83, bf16[6,320,16,64]{1,3,2,0:T(8,128)(2,1)} %copy.78), kind=kOutput, calls=%fused_computation.1 | convolution fusion | flops 1307412480 | bytes 86755200 | tf_op jit(solution)/shard_map/wqhd,wkhd->whqk/dot_general | solution.py:171
  403.4 23.6 %convolution_bitcast_fusion.2 = f32[6,320,16,64]{1,3,2,0:T(8,128)} fusion(bf16[6,320,16,64]{1,3,2,0:T(8,128)(2,1)} %copy.83, f32[6,16,320,320]{2,3,1,0:T(8,128)} %get-tuple-element.57, f32[6,16,320]{2,1,0:T(8,128)S(1)} %log_add_fusion, pred[6,320]{1,0:T(8,128)(4,1)S(1)} %transpose.64), kind=kOutput, calls=%fused_computation.72 | convolution fusion | flops 1297612800 | bytes 51242880 | tf_op jit(solution)/shard_map/whqk,wqhd->wkhd/dot_general | solution.py:184
  427.0 37.7 %multiply_convert_fusion = bf16[6,16,320,320]{2,3,1,0:T(8,128)(2,1)} fusion(f32[6,16,320,320]{2,3,1,0:T(8,128)} %get-tuple-element.63, f32[6,16,320,320]{2,3,1,0:T(8,128)} %get-tuple-element.57, f32[6,16,320]{2,1,0:T(8,128)S(1)} %get-tuple-element.62, f32[6,16,320]{2,1,0:T(8,128)S(1)} %log_add_fusion, pred[6,320]{1,0:T(8,128)(4,1)S(1)} %transpose.64), kind=kLoop, calls=%fused_computation | loop fusion | flops 58982400 | bytes 98551680 | tf_op jit(solution)/shard_map/convert_element_type | solution.py:175
  464.7 20.2 %multiply_bitcast_fusion = f32[6,320,16,64]{1,3,2,0:T(8,128)} fusion(bf16[6,320,16,64]{1,3,2,0:T(8,128)(2,1)} %copy.76, bf16[6,16,320,320]{2,3,1,0:T(8,128)(2,1)} %multiply_convert_fusion), kind=kOutput, calls=%fused_computation.24 | convolution fusion | flops 1260257280 | bytes 31457280 | tf_op jit(solution)/shard_map/whqk,wqhd->wkhd/dot_general | solution.py:181
  484.9 15.7 multiply_bitcast_fusion.1
  500.6 19.3 %convolution_bitcast_fusion.1 = f32[128,32,8,128]{3,2,1,0:T(8,128)} fusion(bf16[1280,4096]{1,0:T(8,128)(2,1)} %get-tuple-element.59, f32[1280,1024]{1,0:T(8,128)} %copy-done.10, f32[1024]{0:T(1024)S(1)} %bitcast.249, f32[1024]{0:T(1024)S(1)} %bitcast.253, f32[1280]{0:T(1024)S(1)} %fusion.48, f32[1280]{0:T(1024)S(1)} %broadcast_multiply_fusion.1), kind=kOutput, calls=%fused_computation.27 | convolution fusion | flops 10743971840 | bytes 32524288 | tf_op jit(solution)/shard_map/dot_general | solution.py:52
  519.9 22.8 %convolution_bitcast_fusion = f32[512,8,8,128]{3,2,1,0:T(8,128)} fusion(bf16[1280,1024]{1,0:T(8,128)(2,1)S(1)} %copy-done.16, f32[1280,4096]{1,0:T(8,128)} %get-tuple-element.60), kind=kOutput, calls=%fused_computation.26 | convolution fusion | flops 10784604160 | bytes 40370176 | tf_op jit(solution)/shard_map/dot_general | solution.py:52
  542.7 13.7 copy.91
  556.5 14.2 reshape_reshape.31
  570.6 7.8 copy.92
  578.4 13.7 copy.95
  592.2 14.2 reshape_reshape.32
  606.3 7.9 copy.96
  614.2 9.6 fusion.9
  633.5 11.2 copy.87
  644.7 11.4 reshape_reshape.30
  671.2 6.9 copy.107
  678.1 15.7 copy.108
  711.3 7.5 fusion.29
  724.9 1046.4 %all-reduce.22 = (bf16[1048576]{0:T(1024)(128)(2,1)}, bf16[1048576]{0:T(1024)(128)(2,1)}, bf16[1048576]{0:T(1024)(128)(2,1)}, bf16[1048576]{0:T(1024)(128)(2,1)S...) all-reduce(f32[1048576]{0:T(1024)} %bitcast.202, ...), channel_id=2, replica_groups=mesh['dp'=16,'band'=2] {'dp'}, use_global_device_ids=true, to_apply=%region_21.22.clone | all-reduce | flops 12582912 | bytes 75497472
  1780.5 5.6 fusion.24
  1786.2 7.5 psum.7
  1793.7 8.2 add_convert_fusion
  1801.9 34.7 %all-reduce.21.cloned.1.call-done = (bf16[65536]{0:T(1024)(128)(2,1)}, bf16[65536]{0:T(1024)(128)(2,1)}, bf16[65536]{0:T(1024)(128)(2,1)}, bf16[65536]{0:T(1024)...) async-done(((bf16[65536]{0:T(1024)(128)(2,1)}, bf16[65536]{0:T(1024)(128)(2,1)}, bf16[65536]{0:T(1024)(128)(2,1)}, bf16[65536]{0:T(1024)(128)(2,1)}, ...) | async-done | bytes 1572880
  1837.6 4.9 all_gather.18
  1863.7 8.6 all_gather.22
  1873.3 7.0 all_gather.23
  (214 shorter events, 135.7 us)
Async XLA Ops:
  7.2 233.6 %copy-start = (bf16[1024,1024]{1,0:T(8,128)(2,1)S(1)}, bf16[1024,1024]{1,0:T(8,128)(2,1)}, u32[]{:S(2)}) copy-start(bf16[1024,1024]{1,0:T(8,128)(2,1)} %param.16) | copy-start | bytes 6291460
  7.2 5.1 copy-start.37
  7.2 6.5 copy-start.26
  7.2 1829.4 %all-reduce.21.cloned.1.call-start = ((), (), s32[]{:S(2)}) async-start(), calls=%async_computation | async-start | bytes 3145728
  12.2 7.6 copy-start.18
  13.7 6.2 copy-start.24
  13.7 6.2 copy-start.20
  13.8 19.5 %copy-start.27 = (f32[1,1,1024]{2,0,1:T(1,128)}, f32[1,1,1024]{2,0,1:T(1,128)S(1)}, u32[]{:S(2)}) copy-start(f32[1,1,1024]{2,0,1:T(1,128)S(1)} %get-tuple-element.50) | copy-start | bytes 12292
  13.8 72.4 %copy-start.22 = (f32[1,1,1024]{2,0,1:T(1,128)}, f32[1,1,1024]{2,0,1:T(1,128)S(1)}, u32[]{:S(2)}) copy-start(f32[1,1,1024]{2,0,1:T(1,128)S(1)} %get-tuple-element.52) | copy-start | bytes 12292
  13.8 236.0 %copy-start.35 = (f32[1,1,1024]{2,0,1:T(1,128)}, f32[1,1,1024]{2,0,1:T(1,128)S(1)}, u32[]{:S(2)}) copy-start(f32[1,1,1024]{2,0,1:T(1,128)S(1)} %get-tuple-element.54) | copy-start | bytes 12292
  13.8 324.9 %copy-start.33 = (f32[1,1,1024]{2,0,1:T(1,128)}, f32[1,1,1024]{2,0,1:T(1,128)S(1)}, u32[]{:S(2)}) copy-start(f32[1,1,1024]{2,0,1:T(1,128)S(1)} %get-tuple-element.53) | copy-start | bytes 12292
  16.7 18.8 slice-start.10
  19.9 15.7 slice-start.11
  23.1 10.2 copy-start.5
  25.7 64.1 %collective-permute-start.1 = (bf16[2,5,4,16,1024]{4,3,2,1,0:T(8,128)(2,1)}, bf16[2,5,4,16,1024]{4,3,2,1,0:T(8,128)(2,1)S(1)}, u32[]{:S(2)}, u32[]{:S(2)}) collective-permute-start(bf16[2,5,4,16,1024]{4,3,2,1,0:T(8,128)(2,1)} %get-tuple-element.47), channel_id=1, source_target_pairs={{1,0},{3,2},{5,4},{7,6},{9,8},{11,10},{13,12},{15,14},{17,16},{19,... | collective-permute-start | bytes 3932168 | tf_op jit(solution)/shard_map/ppermute | solution.py:24
  27.1 62.7 %collective-permute-start = (bf16[2,5,4,16,1024]{4,3,2,1,0:T(8,128)(2,1)}, bf16[2,5,4,16,1024]{4,3,2,1,0:T(8,128)(2,1)}, u32[]{:S(2)}, u32[]{:S(2)}) collective-permute-start(bf16[2,5,4,16,1024]{4,3,2,1,0:T(8,128)(2,1)} %get-tuple-element.46), channel_id=1, source_target_pairs={{0,1},{2,3},{4,5},{6,7},{8,9},{10,11},{12,13},{14,15},{16,17},{18,... | collective-permute-start | bytes 3932168 | tf_op jit(solution)/shard_map/ppermute | solution.py:22
  71.0 11.3 copy-start.44
  71.0 13.2 copy-start.43
  86.1 3.7 copy-start.7
  86.1 4.0 copy-start.9
  240.8 6.0 copy-start.12
  283.3 20.1 %copy-start.28 = (f32[1,1,1024]{2,0,1:T(1,128)S(1)}, f32[1,1,1024]{2,0,1:T(1,128)}, u32[]{:S(2)}) copy-start(f32[1,1,1024]{2,0,1:T(1,128)} %copy-done.27) | copy-start | bytes 12292
  338.7 3.2 copy-start.4
  484.9 15.7 copy-start.36
  500.6 19.3 %copy-start.16 = (bf16[1280,1024]{1,0:T(8,128)(2,1)S(1)}, bf16[1280,1024]{1,0:T(8,128)(2,1)}, u32[]{:S(2)}) copy-start(bf16[1280,1024]{1,0:T(8,128)(2,1)} %copy-done.15) | copy-start | bytes 7864324
  627.5 71.0 %collective-permute-start.3 = (bf16[2,5,4,16,1024]{4,3,2,1,0:T(8,128)(2,1)}, bf16[2,5,4,16,1024]{4,3,2,1,0:T(8,128)(2,1)S(1)}, u32[]{:S(2)}, u32[]{:S(2)}) collective-permute-start(bf16[2,5,4,16,1024]{4,3,2,1,0:T(8,128)(2,1)} %get-tuple-element.37), channel_id=1, source_target_pairs={{1,0},{3,2},{5,4},{7,6},{9,8},{11,10},{13,12},{15,14},{17,16},{19,... | collective-permute-start | bytes 3932168 | tf_op jit(solution)/shard_map/ppermute | solution.py:34
  628.8 69.7 %collective-permute-start.2 = (bf16[2,5,4,16,1024]{4,3,2,1,0:T(8,128)(2,1)}, bf16[2,5,4,16,1024]{4,3,2,1,0:T(8,128)(2,1)S(1)}, u32[]{:S(2)}, u32[]{:S(2)}) collective-permute-start(bf16[2,5,4,16,1024]{4,3,2,1,0:T(8,128)(2,1)} %get-tuple-element.36), channel_id=1, source_target_pairs={{0,1},{2,3},{4,5},{6,7},{8,9},{10,11},{12,13},{14,15},{16,17},{18,... | collective-permute-start | bytes 3932168 | tf_op jit(solution)/shard_map/ppermute | solution.py:34
  658.8 6.4 slice-start.4
  659.0 6.2 slice-start.5
  662.0 9.2 slice-start.6
  665.2 6.0 slice-start.7
  665.2 6.0 slice-start.8
  665.2 6.0 slice-start.9
  678.1 20.4 %slice-start.2 = ((s8[7864320]{0:T(1024)(128)(4,1)}), s8[4194304]{0:T(1024)(128)(4,1)S(1)}, s32[]{:S(2)}) async-start(s8[7864320]{0:T(1024)(128)(4,1)} %bitcast.193), calls=%async_computation.3 | async-start | bytes 8388608
  678.1 15.7 copy-start.38
  678.1 20.4 %slice-start.3 = ((s8[7864320]{0:T(1024)(128)(4,1)}), s8[3670016]{0:T(1024)(128)(4,1)S(1)}, s32[]{:S(2)}) async-start(s8[7864320]{0:T(1024)(128)(4,1)} %bitcast.193), calls=%async_computation.4 | async-start | bytes 7340032
  693.8 4.7 slice-start
  693.8 4.7 slice-start.1
  700.7 10.6 slice-start.12
  703.6 7.6 slice-start.13
  711.3 7.5 copy-start.25
  724.9 1055.6 %copy-start.21 = (f32[1280]{0:T(1024)S(1)}, f32[1280]{0:T(1024)}, u32[]{:S(2)}) copy-start(f32[1280]{0:T(1024)} %copy-done.20) | copy-start | bytes 15364
  1778.6 7.5 copy-start.29
  1778.6 7.5 copy-start.30
  1778.6 7.5 copy-start.31
  1778.6 7.5 copy-start.32
  1793.7 87.7 %copy-start.1 = (bf16[1024,1024]{1,0:T(8,128)(2,1)S(1)}, bf16[1024,1024]{1,0:T(8,128)(2,1)}, u32[]{:S(2)}) copy-start(bf16[1024,1024]{1,0:T(8,128)(2,1)} %param.16) | copy-start | bytes 6291460
  1836.7 36.6 %copy-start.17 = (bf16[262144]{0:T(1024)(128)(2,1)S(1)}, bf16[262144]{0:T(1024)(128)(2,1)}, u32[]{:S(2)}) copy-start(bf16[262144]{0:T(1024)(128)(2,1)} %get-tuple-element.29) | copy-start | bytes 1572868
  (16 other events, 46.2 us)
Sparse Core Ops, SparseCore 0:
  1780.6 56.0 all-reduce.20
where the time goes:
time: 1900 us; the launch traced here: 1890 us
  blocking collectives  1090 us (57%)
  matrix products  331 us (17%)
  local copies, waits for them, and re-layouts  287 us (15%)
  other arithmetic  113 us (6%)
  waiting for transfers between devices  34.8 us (2%)
  between operations  20 us (1%)
    unnamed x1, blocking collectives  1050 us
    another operation x8, local copies, waits for them, and re-layouts, windowed(): return windows.reshape(windows.shape[0], windows.shape[1], HEADS, HEAD_DIM)  90.2 us
    dot_general x6, matrix products, matmul(): return jnp.dot(left, right, preferred_element_type=jnp.float32)  79.8 us
    unnamed x138, local copies, waits for them, and re-layouts  54.7 us
    dot_general x6, matrix products, back_product(): lax.dot_general(left, right, (((1,), (1,)), ((), ())), preferred_element_...  54.5 us
    dot_general x6, matrix products, outer_sum(): lax.dot_general(left, right, (((0,), (0,)), ((), ())), preferred_element_...  53.8 us
    another operation x4, local copies, waits for them, and re-layouts, from_windows(): windows.reshape(row_count // 8, col_count // 8, frame_count, 8, 8, model_...  51.1 us
  transfers between devices with their start and end apart: 5, of which 1 were waited for; matrix products, arithmetic and copies ran while one was open for 7% of the time, Pallas kernels for 0%

commit v1 on v0

v1 whole, which is shorter than its diff:
```python
import functools

import jax
import jax.numpy as jnp
from jax import lax
from jax.experimental import pallas as pl
from jax.experimental.pallas import tpu as pltpu
from jax.sharding import PartitionSpec as P

HEADS = 16
HEAD_DIM = 64
EPS = 1e-06
MASKED = -1e30
LOG2E = 1.4426950408889634
F32 = jnp.float32
BF16 = jnp.bfloat16
ANY = pl.BlockSpec(memory_space=pl.ANY)
VMEM_LIMIT = 60 * 1024 * 1024

MID_SPOTS = ((1, 0), (2, 0), (1, 1), (2, 1))


def group_spot(band, s):
    lone = 3 * band
    paired = 3 - 3 * band
    if s < 2:
        return lone, s
    if s < 6:
        return MID_SPOTS[s - 2]
    return paired, s - 6


def params(**kw):
    return pltpu.CompilerParams(vmem_limit_bytes=VMEM_LIMIT, **kw)


def dot(a, b, ca=1, cb=0):
    return lax.dot_general(a, b, (((ca,), (cb,)), ((), ())), preferred_element_type=F32)


def whole(shape):
    return pl.BlockSpec(shape, lambda *_: (0,) * len(shape), pipeline_mode=pl.Buffered(1))


def norm_stats(v):
    c = v - jnp.mean(v, axis=-1, keepdims=True)
    r = lax.rsqrt(jnp.mean(c * c, axis=-1, keepdims=True) + EPS)
    return c * r, r


def spot_copy(hbm, vmem, band, s, sem, out=False):
    g, j = group_spot(band, s)
    there = hbm.at[0, :, pl.ds(g * 4, 4), pl.ds(j * 8, 8), :]
    if out:
        return pltpu.make_async_copy(vmem.at[s], there, sem.at[s])
    return pltpu.make_async_copy(there, vmem.at[s], sem.at[s])


def pre_kernel(n_group, from_spots, x_hbm, mod_ref, *refs):
    n_mat = (len(refs) - 5) // 2 if from_spots else (len(refs) - 3) // 2
    w_refs = refs[:n_mat]
    outs = refs[n_mat:]
    if from_spots:
        xw_ref, normed_ref = outs[:2]
        o_refs = outs[2 : 2 + n_mat]
    else:
        o_refs = outs[:n_mat]
    stage, sem, nsc = outs[-3:] if not from_spots else outs[-3:]
    rows = nsc.shape[0] // n_group

    @pl.when(pl.program_id(0) == 0)
    def _():
        band = lax.axis_index("band")
        if from_spots:
            copies = [spot_copy(x_hbm, stage, band, s, sem) for s in range(n_group)]
        else:
            copies = [
                pltpu.make_async_copy(x_hbm.at[:, :, pl.ds(8 * s, 8), :], stage.at[s], sem.at[s])
                for s in range(n_group)
            ]
        for c in copies:
            c.start()
        for s in range(n_group):
            copies[s].wait()
            x = stage[s].astype(F32).reshape(rows, stage.shape[-1])
            n, _ = norm_stats(x)
            part = pl.ds(s * rows, rows)
            nsc[part, :] = (n * (1.0 + mod_ref[1:2, :]) + mod_ref[0:1, :]).astype(BF16)
            if from_spots:
                xw_ref[part, :] = x.astype(BF16)
                normed_ref[part, :] = nsc[part, :]

    for w_ref, o_ref in zip(w_refs, o_refs):
        o_ref[...] = dot(nsc[...], w_ref[...]).astype(BF16)


def pre(x, mod, weights, n_group, from_spots):
    d = x.shape[-1]
    frames = x.shape[1] if from_spots else x.shape[0]
    rows = frames * 32
    t = n_group * rows
    tile = 256
    o_tile = pl.BlockSpec((t, tile), lambda n: (0, n))
    full = pl.BlockSpec((t, d), lambda n: (0, 0))
    act = jax.ShapeDtypeStruct((t, d), BF16)
    k = len(weights)
    head = [act, act] if from_spots else []
    return pl.pallas_call(
        functools.partial(pre_kernel, n_group, from_spots),
        grid=(d // tile,),
        in_specs=[ANY, whole((6, d))] + [pl.BlockSpec((d, tile), lambda n: (0, n))] * k,
        out_specs=[full] * len(head) + [o_tile] * k,
        out_shape=head + [act] * k,
        scratch_shapes=[
            pltpu.VMEM((n_group, frames, 4, 8, d), BF16),
            pltpu.SemaphoreType.DMA((n_group,)),
            pltpu.VMEM((t, d), BF16),
        ],
        compiler_params=params(),
        name="pre" if from_spots else "pre_halo",
        cost_estimate=pl.CostEstimate(
            flops=2 * t * d * d * k, bytes_accessed=2 * (k * d * d + (k + 3) * t * d), transcendentals=0
        ),
    )(x, mod, *weights)


def units(rows):
    r = rows
    out = [((0, r), (0, r), None), ((r, r), (r, r), None)]
    out += [((2 * r, 2 * r), (2 * r, 2 * r), None), ((4 * r, 2 * r), (4 * r, 2 * r), None)]
    out += [((6 * r, r), (6 * r, r), (0, r)), ((7 * r, r), (7 * r, r), (r, r))]
    return out


SCALE2 = HEAD_DIM**-0.5 * LOG2E


def attn_fwd_kernel(ok_ref, q_ref, k_ref, v_ref, kh_ref, vh_ref, o_ref, lse_ref):
    r = q_ref.shape[0] // 8
    halo_ok = ok_ref[0] == 1
    for h in range(2):
        lanes = slice(64 * h, 64 * h + 64)
        for (q0, qn), (k0, kn), halo in units(r):
            q = q_ref[q0 : q0 + qn, lanes]
            k = k_ref[k0 : k0 + kn, lanes]
            v = v_ref[k0 : k0 + kn, lanes]
            s = dot(q, k, 1, 1) * SCALE2
            top = jnp.max(s, axis=-1, keepdims=True)
            if halo is not None:
                kh = kh_ref[halo[0] : halo[0] + halo[1], lanes]
                vh = vh_ref[halo[0] : halo[0] + halo[1], lanes]
                sh = jnp.where(halo_ok, dot(q, kh, 1, 1) * SCALE2, MASKED)
                top = jnp.maximum(top, jnp.max(sh, axis=-1, keepdims=True))
            e = jnp.exp2(s - top)
            total = jnp.sum(e, axis=-1, keepdims=True)
            o = dot(e.astype(BF16), v)
            if halo is not None:
                eh = jnp.exp2(sh - top)
                total = total + jnp.sum(eh, axis=-1, keepdims=True)
                o = o + dot(eh.astype(BF16), vh)
            o_ref[q0 : q0 + qn, lanes] = (o * (1.0 / total)).astype(BF16)
            lse_ref[q0 : q0 + qn, lanes] = jnp.broadcast_to(top + jnp.log2(total), (qn, 64))


def attn_fwd(halo_ok, q, k, v, kh, vh):
    t, d = q.shape
    th = kh.shape[0]
    big = pl.BlockSpec((t, 128), lambda n: (0, n))
    small = pl.BlockSpec((th, 128), lambda n: (0, n))
    pairs = t * t // 8 * 2 * 7 // 8
    return pl.pallas_call(
        attn_fwd_kernel,
        grid=(d // 128,),
        in_specs=[pl.BlockSpec(memory_space=pltpu.SMEM), big, big, big, small, small],
        out_specs=[big, big],
        out_shape=[jax.ShapeDtypeStruct((t, d), BF16), jax.ShapeDtypeStruct((t, d), F32)],
        compiler_params=params(),
        name="attn_fwd",
        cost_estimate=pl.CostEstimate(
            flops=4 * pairs * d * 4, bytes_accessed=12 * t * d, transcendentals=pairs * 16
        ),
    )(halo_ok, q, k, v, kh, vh)


def attn_bwd_kernel(which, ok_ref, q_ref, k_ref, v_ref, do_ref, lse_ref, *refs):
    base = 0
    if which == "paired":
        kh_ref, vh_ref, dq_ref, dk_ref, dv_ref, out_ref = refs
        r = q_ref.shape[0] // 2
        base = 6 * r
        todo = units(r)[4:]
        halo_ok = ok_ref[0] == 1
    else:
        dq_ref, dk_ref, dv_ref = refs
        r = q_ref.shape[0] // 6
        todo = units(r)[:4]
    scale = HEAD_DIM**-0.5
    for h in range(2):
        lanes = slice(64 * h, 64 * h + 64)
        for (q0, qn), (k0, kn), halo in todo:
            qs, ks = slice(q0 - base, q0 - base + qn), slice(k0 - base, k0 - base + kn)
            q, k, v = q_ref[qs, lanes], k_ref[ks, lanes], v_ref[ks, lanes]
            do = do_ref[qs, lanes]
            lse = lse_ref[qs, 64 * h : 64 * h + 1]
            p = jnp.exp2(dot(q, k, 1, 1) * SCALE2 - lse)
            dp = dot(do, v, 1, 1)
            row = jnp.sum(p * dp, axis=-1, keepdims=True)
            if halo is not None:
                hs = slice(halo[0], halo[0] + halo[1])
                kh, vh = kh_ref[hs, lanes], vh_ref[hs, lanes]
                sh = jnp.where(halo_ok, dot(q, kh, 1, 1) * SCALE2, MASKED)
                ph = jnp.exp2(sh - lse)
                dph = dot(do, vh, 1, 1)
                row = row + jnp.sum(ph * dph, axis=-1, keepdims=True)
            ds = (p * (dp - row)).astype(BF16)
            dq = dot(ds, k)
            dk = dot(ds, q, 0, 0) * scale
            dv = dot(p.astype(BF16), do, 0, 0)
            if halo is not None:
                dsh = (ph * (dph - row)).astype(BF16)
                dq = dq + dot(dsh, kh)
                out_ref[0, hs, lanes] = (dot(dsh, q, 0, 0) * scale).astype(BF16)
                out_ref[1, hs, lanes] = dot(ph.astype(BF16), do, 0, 0).astype(BF16)
            dq_ref[qs, lanes] = (dq * scale).astype(dq_ref.dtype)
            dk_ref[ks, lanes] = dk.astype(dk_ref.dtype)
            dv_ref[ks, lanes] = dv.astype(dv_ref.dtype)


def attn_bwd_main(halo_ok, q, k, v, do, lse):
    t, d = q.shape
    part = t // 8 * 6
    big = pl.BlockSpec((part, 128), lambda n: (0, n))
    act = jax.ShapeDtypeStruct((t, d), BF16)
    pairs = t * t // 64 * 10
    return pl.pallas_call(
        functools.partial(attn_bwd_kernel, "main"),
        grid=(d // 128,),
        in_specs=[pl.BlockSpec(memory_space=pltpu.SMEM)] + [big] * 5,
        out_specs=[big] * 3,
        out_shape=[jax.ShapeDtypeStruct((part, d), BF16)] * 3,
        compiler_params=params(),
        name="attn_bwd_main",
        cost_estimate=pl.CostEstimate(
            flops=10 * pairs * d * 4, bytes_accessed=18 * t * d, transcendentals=pairs * 16
        ),
    )(halo_ok, q, k, v, do, lse)


def attn_bwd_paired(halo_ok, q, k, v, do, lse, kh, vh):
    t, d = q.shape
    part = t // 4
    big = pl.BlockSpec((part, 128), lambda n: (3, n))
    small = pl.BlockSpec((part, 128), lambda n: (0, n))
    f32 = jax.ShapeDtypeStruct((part, d), F32)
    pairs = t * t // 64 * 4
    return pl.pallas_call(
        functools.partial(attn_bwd_kernel, "paired"),
        grid=(d // 128,),
        in_specs=[pl.BlockSpec(memory_space=pltpu.SMEM)] + [big] * 5 + [small] * 2,
        out_specs=[small] * 3 + [pl.BlockSpec((2, part, 128), lambda n: (0, 0, n))],
        out_shape=[jax.ShapeDtypeStruct((part, d), BF16), f32, f32, jax.ShapeDtypeStruct((2, part, d), BF16)],
        compiler_params=params(),
        name="attn_bwd_paired",
        cost_estimate=pl.CostEstimate(
            flops=10 * pairs * d * 4, bytes_accessed=12 * t * d, transcendentals=pairs * 16
        ),
    )(halo_ok, q, k, v, do, lse, kh, vh)


def mid_kernel(g_hbm, live_ref, att_ref, w_ref, x_ref, mod_ref, ao_ref, mid_ref, nm_ref, gw_ref, gm_ref, stage, sem):
    step = pl.program_id(0)
    band = lax.axis_index("band")
    live = live_ref[0].astype(F32)
    n_group = stage.shape[0]
    per = n_group // 4
    rows = gw_ref.shape[0] // per

    @pl.when(step == 0)
    def _():
        for s in range(n_group):
            spot_copy(g_hbm, stage, band, s, sem).start()

    attn_out = dot(att_ref[...], w_ref[...])
    middle = x_ref[...].astype(F32) + (live * mod_ref[2:3, :]) * attn_out
    ao_ref[...] = attn_out
    mid_ref[...] = middle
    n, _ = norm_stats(middle)
    nm_ref[...] = (n * (1.0 + mod_ref[4:5, :]) + mod_ref[3:4, :]).astype(BF16)
    for i in range(per):
        s = step * per + i
        pltpu.make_async_copy(g_hbm.at[0, :, pl.ds(0, 4), pl.ds(0, 8), :], stage.at[s], sem.at[s]).wait()
        g = stage[s].astype(F32).reshape(rows, stage.shape[-1])
        part = pl.ds(i * rows, rows)
        gw_ref[part, :] = g.astype(BF16)
        gm_ref[part, :] = ((live * mod_ref[5:6, :]) * g).astype(BF16)


def mid(cot, live, attended, w_out, xw, mod):
    t, d = xw.shape
    frames = cot.shape[1]
    blk = pl.BlockSpec((t // 4, d), lambda m: (m, 0))
    bf, f32 = jax.ShapeDtypeStruct((t, d), BF16), jax.ShapeDtypeStruct((t, d), F32)
    return pl.pallas_call(
        mid_kernel,
        grid=(4,),
        in_specs=[ANY, pl.BlockSpec(memory_space=pltpu.SMEM), blk, whole((d, d)), blk, whole((6, d))],
        out_specs=[blk] * 5,
        out_shape=[f32, f32, bf, bf, bf],
        scratch_shapes=[pltpu.VMEM((8, frames, 4, 8, d), BF16), pltpu.SemaphoreType.DMA((8,))],
        compiler_params=params(),
        name="mid",
        cost_estimate=pl.CostEstimate(flops=2 * t * d * d, bytes_accessed=22 * t * d, transcendentals=0),
    )(cot, live, attended, w_out, xw, mod)


GELU_C = 0.7978845608
GELU_A = 0.044715


def mlp_kernel(nm_ref, gm_ref, wu_ref, wd_ref, mo_ref, h_ref, dwu_ref, dwd_ref, hid, gp):
    first = pl.program_id(0) == 0
    t = nm_ref.shape[0]
    chunk = t // 4

    @pl.when(first)
    def _():
        mo_ref[...] = jnp.zeros_like(mo_ref)
        h_ref[...] = jnp.zeros_like(h_ref)

    def rows(i, _):
        part = pl.ds(pl.multiple_of(i * chunk, chunk), chunk)
        nm, gm = nm_ref[part, :], gm_ref[part, :]
        v = dot(nm, wu_ref[...])
        gh = dot(gm, wd_ref[...], 1, 1)
        v2 = v * v
        th = jnp.tanh(v * (GELU_C + (GELU_C * GELU_A) * v2))
        half = 0.5 * th + 0.5
        hidden = (v * half).astype(BF16)
        slope = half + (0.5 * v) * (1.0 - th * th) * (GELU_C + (3.0 * GELU_C * GELU_A) * v2)
        gpre = (gh * slope).astype(BF16)
        hid[part, :] = hidden
        gp[part, :] = gpre
        mo_ref[part, :] += dot(hidden, wd_ref[...])
        h_ref[part, :] += dot(gpre, wu_ref[...], 1, 1)
        return 0

    lax.fori_loop(0, 4, rows, 0)
    dwd_ref[...] = dot(hid[...], gm_ref[...], 0, 0).astype(BF16)
    dwu_ref[...] = dot(nm_ref[...], gp[...], 0, 0).astype(BF16)


def mlp(nm, gm, w_up, w_down):
    t, d = nm.shape
    ff = w_up.shape[1]
    tile = 512
    f32 = jax.ShapeDtypeStruct((t, d), F32)
    return pl.pallas_call(
        mlp_kernel,
        grid=(ff // tile,),
        in_specs=[
            whole((t, d)),
            whole((t, d)),
            pl.BlockSpec((d, tile), lambda f: (0, f)),
            pl.BlockSpec((tile, d), lambda f: (f, 0)),
        ],
        out_specs=[
            whole((t, d)),
            whole((t, d)),
            pl.BlockSpec((d, tile), lambda f: (0, f)),
            pl.BlockSpec((tile, d), lambda f: (f, 0)),
        ],
        out_shape=[f32, f32, jax.ShapeDtypeStruct((d, ff), BF16), jax.ShapeDtypeStruct((ff, d), BF16)],
        scratch_shapes=[pltpu.VMEM((t, tile), BF16), pltpu.VMEM((t, tile), BF16)],
        compiler_params=params(),
        name="mlp",
        cost_estimate=pl.CostEstimate(flops=12 * t * d * ff, bytes_accessed=8 * d * ff + 12 * t * d, transcendentals=t * ff),
    )(nm, gm, w_up, w_down)


def post_kernel(live_ref, mid_ref, mo_ref, h_ref, g_ref, ao_ref, mod_ref, w_ref, out_hbm, gmid_ref, ga_ref, do_ref, sums_ref, stage, sem):
    step = pl.program_id(0)
    band = lax.axis_index("band")
    live = live_ref[0].astype(F32)
    n_group = stage.shape[0]
    per = n_group // 4
    middle = mid_ref[...]
    g = g_ref[...].astype(F32)
    mo = mo_ref[...]
    h = h_ref[...]
    out = middle + (live * mod_ref[5:6, :]) * mo
    n, r = norm_stats(middle)
    e = h * (1.0 + mod_ref[4:5, :])
    gmid = g + r * (e - jnp.mean(e, axis=-1, keepdims=True) - n * jnp.mean(e * n, axis=-1, keepdims=True))
    gmid_ref[...] = gmid
    ga = ((live * mod_ref[2:3, :]) * gmid).astype(BF16)
    ga_ref[...] = ga
    do_ref[...] = dot(ga, w_ref[...], 1, 1).astype(BF16)

    def col(v):
        return jnp.sum(v, axis=0, keepdims=True)

    sums = jnp.concatenate(
        [col(live * ao_ref[...] * gmid), col(h), col(h * n), col(live * mo * g), jnp.zeros((4, h.shape[1]), F32)], axis=0
    )

    @pl.when(step == 0)
    def _():
        sums_ref[...] = sums

    @pl.when(step > 0)
    def _():
        sums_ref[...] += sums

    rows = h.shape[0] // per
    shape = stage.shape[1:]
    for k in range(4):

        @pl.when(step == k)
        def _():
            for i in range(per):
                s = k * per + i
                stage[s] = out[i * rows : (i + 1) * rows, :].reshape(shape).astype(BF16)
                spot_copy(out_hbm, stage, band, s, sem, out=True).start()

    @pl.when(step == 3)
    def _():
        for s in range(n_group):
            spot_copy(out_hbm, stage, band, s, sem, out=True).wait()


def post(live, middle, mo, h, gw, ao, mod, w_out, like):
    t, d = gw.shape
    frames = like.shape[1]
    blk = pl.BlockSpec((t // 4, d), lambda m: (m, 0))
    bf, f32 = jax.ShapeDtypeStruct((t, d), BF16), jax.ShapeDtypeStruct((t, d), F32)
    return pl.pallas_call(
        post_kernel,
        grid=(4,),
        in_specs=[pl.BlockSpec(memory_space=pltpu.SMEM), blk, blk, blk, blk, blk, whole((6, d)), whole((d, d))],
        out_specs=[ANY, blk, blk, blk, pl.BlockSpec((8, d), lambda m: (0, 0))],
        out_shape=[jax.ShapeDtypeStruct(like.shape, BF16), f32, bf, bf, jax.ShapeDtypeStruct((8, d), F32)],
        scratch_shapes=[pltpu.VMEM((8, frames, 4, 8, d), BF16), pltpu.SemaphoreType.DMA((8,))],
        compiler_params=params(),
        name="post",
        cost_estimate=pl.CostEstimate(flops=2 * t * d * d, bytes_accessed=30 * t * d, transcendentals=0),
    )(live, middle, mo, h, gw, ao, mod, w_out)


def outer_kernel(a_ref, b_ref, o_ref):
    o_ref[...] = dot(a_ref[...], b_ref[...], 0, 0).astype(BF16)


def outer(a, b):
    t, d = a.shape
    tile = 512
    return pl.pallas_call(
        outer_kernel,
        grid=(b.shape[1] // tile,),
        in_specs=[whole((t, d)), pl.BlockSpec((t, tile), lambda n: (0, n))],
        out_specs=pl.BlockSpec((d, tile), lambda n: (0, n)),
        out_shape=jax.ShapeDtypeStruct((d, b.shape[1]), BF16),
        compiler_params=params(),
        name="outer",
        cost_estimate=pl.CostEstimate(flops=2 * t * d * b.shape[1], bytes_accessed=6 * t * d, transcendentals=0),
    )(a, b)


def final_kernel(dq_ref, dk_ref, dv_ref, wq_ref, wk_ref, wv_ref, x_ref, gmid_ref, mod_ref, out_hbm, sums_ref, stage, sem):
    step = pl.program_id(0)
    band = lax.axis_index("band")
    n_group = stage.shape[0]
    per = n_group // 4
    h = dot(dq_ref[...], wq_ref[...], 1, 1) + dot(dk_ref[...], wk_ref[...], 1, 1) + dot(dv_ref[...], wv_ref[...], 1, 1)
    n, r = norm_stats(x_ref[...].astype(F32))
    e = h * (1.0 + mod_ref[1:2, :])
    out = gmid_ref[...] + r * (e - jnp.mean(e, axis=-1, keepdims=True) - n * jnp.mean(e * n, axis=-1, keepdims=True))

    def col(v):
        return jnp.sum(v, axis=0, keepdims=True)

    sums = jnp.concatenate([col(h), col(h * n), jnp.zeros((6, h.shape[1]), F32)], axis=0)

    @pl.when(step == 0)
    def _():
        sums_ref[...] = sums

    @pl.when(step > 0)
    def _():
        sums_ref[...] += sums

    rows = h.shape[0] // per
    shape = stage.shape[1:]
    for k in range(4):

        @pl.when(step == k)
        def _():
            for i in range(per):
                s = k * per + i
                stage[s] = out[i * rows : (i + 1) * rows, :].reshape(shape).astype(BF16)
                spot_copy(out_hbm, stage, band, s, sem, out=True).start()

    @pl.when(step == 3)
    def _():
        for s in range(n_group):
            spot_copy(out_hbm, stage, band, s, sem, out=True).wait()


def final(dq, dk, dv, wq, wk, wv, xw, gmid, mod, like):
    t, d = xw.shape
    frames = like.shape[1]
    blk = pl.BlockSpec((t // 4, d), lambda m: (m, 0))
    return pl.pallas_call(
        final_kernel,
        grid=(4,),
        in_specs=[blk, blk, blk, whole((d, d)), whole((d, d)), whole((d, d)), blk, blk, whole((6, d))],
        out_specs=[ANY, pl.BlockSpec((8, d), lambda m: (0, 0))],
        out_shape=[jax.ShapeDtypeStruct(like.shape, BF16), jax.ShapeDtypeStruct((8, d), F32)],
        scratch_shapes=[pltpu.VMEM((8, frames, 4, 8, d), BF16), pltpu.SemaphoreType.DMA((8,))],
        compiler_params=params(),
        name="final",
        cost_estimate=pl.CostEstimate(flops=6 * t * d * d, bytes_accessed=14 * t * d, transcendentals=0),
    )(dq, dk, dv, wq, wk, wv, xw, gmid, mod)


def band_swap(v):
    return lax.ppermute(v, "band", [(0, 1), (1, 0)])


def reduced(grad):
    share = lax.psum_scatter(grad, "dp", scatter_dimension=0, tiled=True)
    return (share.astype(F32) + band_swap(share).astype(F32)).reshape(-1)


def on_device(
    block_input, modulation, band_live, w_query, w_key, w_value, w_out, w_up, w_down, cotangent
):
    assert lax.axis_size("band") == 2 and block_input.shape[2:4] == (16, 16)
    band = lax.axis_index("band")
    flags = band_live[0]
    live_own = lax.dynamic_index_in_dim(flags, band, keepdims=True)
    live_other = lax.dynamic_index_in_dim(flags, 1 - band, keepdims=True)
    live = (live_own == 1).astype(jnp.int32)
    halo_ok = ((live_other == 1) | (live_own != 1)).astype(jnp.int32)
    mod = modulation[0]

    edge = lax.dynamic_slice_in_dim(block_input[0], 12 - 12 * band, 4, axis=1)
    x_halo = band_swap(edge)
    xw, normed, q, k, v = pre(block_input, mod, (w_query, w_key, w_value), 8, True)
    kh, vh = pre(x_halo, mod, (w_key, w_value), 2, False)
    attended, lse = attn_fwd(halo_ok, q, k, v, kh, vh)
    ao, middle, nm, gw, gm = mid(cotangent, live, attended, w_out, xw, mod)
    mo, h, d_up, d_down = mlp(nm, gm, w_up, w_down)
    g_up, g_down = reduced(d_up), reduced(d_down)
    block_output, gmid, ga, do, sums_m = post(live, middle, mo, h, gw, ao, mod, w_out, block_input)
    g_out = reduced(outer(attended, ga))
    dq2, dk2, dv2, send = attn_bwd_paired(halo_ok, q, k, v, do, lse, kh, vh)
    got = band_swap(send).astype(F32)
    dq1, dk1, dv1 = attn_bwd_main(halo_ok, q, k, v, do, lse)
    dq = jnp.concatenate([dq1, dq2])
    dk = jnp.concatenate([dk1, (dk2 + got[0]).astype(BF16)])
    dv = jnp.concatenate([dv1, (dv2 + got[1]).astype(BF16)])
    g_query, g_key, g_value = (reduced(outer(normed, d)) for d in (dq, dk, dv))
    grad_input, sums_a = final(dq, dk, dv, w_query, w_key, w_value, xw, gmid, mod, block_input)
    mod_part = jnp.concatenate([sums_a[0:2], sums_m[0:4]])
    mod_total = mod_part + band_swap(mod_part)
    return block_output, grad_input, mod_total[None], g_query, g_key, g_value, g_out, g_up, g_down


def solution(mesh):
    return jax.shard_map(
        on_device,
        mesh=mesh,
        in_specs=(
            P("dp", None, "band", None, None),
            P("dp", None, None),
            P("dp", None),
            P(),
            P(),
            P(),
            P(),
            P(),
            P(),
            P("dp", None, "band", None, None),
        ),
        out_specs=(
            P("dp", None, "band", None, None),
            P("dp", None, "band", None, None),
            P("dp", None, None),
            P("dp"),
            P("dp"),
            P("dp"),
            P("dp"),
            P("dp"),
            P("dp"),
        ),
        check_vma=False,
    )
```

time: 1900 us -> 682 us (0.36)
  blocking collectives: 1090 us -> 0 us
  matrix products: 331 us -> 0 us
  waiting for transfers between devices: 34.8 us -> 365 us
  local copies, waits for them, and re-layouts: 287 us -> 17.8 us
  Pallas kernels: 0 us -> 261 us
  other arithmetic: 113 us -> 8.69 us
    unnamed x1 -> x0, blocking collectives: 1050 us -> none
    dot_general x24 -> x0, matrix products: 331 us -> none  [the longest x6 79.8 us: matmul(): return jnp.dot(left, right, preferred_element_type=jnp.float32)]
    reduce_scatter x0 -> x6, waiting for transfers between devices: none -> 323 us  [reduced(): share = lax.psum_scatter(grad, 'dp', scatter_dimension=0, tiled=True)]
    pallas_call x0 -> x13, Pallas kernels: none -> 261 us  [the longest x1 81.5 us: mlp(): pl.pallas_call(mlp_kernel, grid=(ff // tile,), in_specs=[whole((t, d)), w...]
    another operation x14 -> x0, local copies, waits for them, and re-layouts: 141 us -> none  [the longest x8 90.2 us: windowed(): return windows.reshape(windows.shape[0], windows.shape[1], HEADS, HEAD_DIM)]
    transpose x12 -> x0, local copies, waits for them, and re-layouts: 57.7 us -> none  [the longest x4 21 us: from_windows(): blocks = blocks.transpose(2, 0, 3, 1, 4, 5)]
    convert_element_type x11 -> x2, other arithmetic: 58.3 us -> 0.96 us  [the longest x1 0.65 us: on_device(): dv = jnp.concatenate([dv1, (dv2 + got[1]).astype(BF16)])]
    unnamed x138 -> x27, local copies, waits for them, and re-layouts: 54.7 us -> 13.5 us
  transfers between devices with their start and end apart: 5 -> 15, of which waited for: 1 -> 8; matrix products, arithmetic and copies ran while one was open for 7% -> 3% of each run, Pallas kernels for 0% -> 16%
where the time goes in v1:
time: 682 us; the launch traced here: 681 us
  waiting for transfers between devices  365 us (54%)
  Pallas kernels  261 us (38%)
  local copies, waits for them, and re-layouts  17.8 us (3%)
  between operations  16.3 us (2%)
  starting transfers between devices  11.9 us (2%)
  other arithmetic  8.69 us (1%)
    reduce_scatter x6, waiting for transfers between devices, reduced(): share = lax.psum_scatter(grad, 'dp', scatter_dimension=0, tiled=True)  323 us
    pallas_call x1, Pallas kernels, mlp(): pl.pallas_call(mlp_kernel, grid=(ff // tile,), in_specs=[whole((t, d)), w...  81.5 us
    ppermute x9, waiting for transfers between devices, band_swap(): return lax.ppermute(v, 'band', [(0, 1), (1, 0)])  40.9 us
    pallas_call x1, Pallas kernels, attn_bwd_main(): pl.pallas_call(functools.partial(attn_bwd_kernel, 'main'), grid=(d // 128...  35.5 us
    pallas_call x1, Pallas kernels, attn_fwd(): pl.pallas_call(attn_fwd_kernel, grid=(d // 128,), in_specs=[pl.BlockSpec(...  28.5 us
    pallas_call x4, Pallas kernels, outer(): pl.pallas_call(outer_kernel, grid=(b.shape[1] // tile,), in_specs=[whole(...  25.3 us
    pallas_call x2, Pallas kernels, pre(): pl.pallas_call(functools.partial(pre_kernel, n_group, from_spots), grid=(...  21.9 us
    pallas_call x1, Pallas kernels, attn_bwd_paired(): pl.pallas_call(functools.partial(attn_bwd_kernel, 'paired'), grid=(d // 1...  21.3 us
  transfers between devices with their start and end apart: 15, of which 8 were waited for; matrix products, arithmetic and copies ran while one was open for 3% of the time, Pallas kernels for 16%

profile of v1, /device:TPU:0, one launch (start us, length us, event | category | flops | bytes accessed | tf_op | source)
XLA Modules:
  0.0 680.8 jit_solution(724750584171985566)
XLA Ops:
  7.2 1.1 dynamic-slice_bitcast_fusion
  8.4 3.0 collective-permute-start
  11.4 1.3 constant_dynamic-slice_fusion
  14.7 1.4 copy.28
  16.0 15.2 %pre.1 = (bf16[1280,1024]{1,0:T(8,128)(2,1)}, bf16[1280,1024]{1,0:T(8,128)(2,1)}, bf16[1280,1024]{1,0:T(8,128)(2,1)}, bf16[1280,1024]{1,0:T(8,128)(2,1)}, bf16[1280,1024]{1,0:T(8,128)(2,1)}) custom-call(bf16[1,5,16,16,1024]{4,3,2,1,0:T(8,128)(2,1)} %x_hbm.1, f32[6,1024]{1,0:T(8,128)} %bitcast.41, bf16[1024,1024]{1,0:T(8,128)(2,1)} %wq_ref.1, ...), custom_call_target="tpu_custom_call" | custom-call | flops 8053063680 | bytes 22020096 | tf_op jit(solution)/shard_map/pre/pallas_call | solution.py:108
  31.2 0.8 copy-done.8
  32.1 6.7 pre_halo.1
  38.8 28.5 %attn_fwd.1 = (bf16[1280,1024]{1,0:T(8,128)(2,1)}, f32[1280,1024]{1,0:T(8,128)}) custom-call(s32[1]{0:T(128)} %bitcast.1.ok_ref, bf16[1280,1024]{1,0:T(8,128)(2,1)} %get-tuple-element.41.q_ref, bf16[1280,1024]{1,0:T(8,128)(2,1)} %get-tuple-element.42.k_ref, bf16[1280,1024]{1,0:T(8,128)(2,1)} %get-tuple-element.43.v_ref, ...), custom_call_target="tpu_custom_call" | custom-call | flops 5872025600 | bytes 15728640 | tf_op jit(solution)/shard_map/attn_fwd/pallas_call | solution.py:171
  67.3 11.1 %mid.1 = (f32[1280,1024]{1,0:T(8,128)}, f32[1280,1024]{1,0:T(8,128)}, bf16[1280,1024]{1,0:T(8,128)(2,1)}, bf16[1280,1024]{1,0:T(8,128)(2,1)}, bf16[1280,1024]{1,0:T(8,128)(2,1)}) custom-call(bf16[1,5,16,16,1024]{4,3,2,1,0:T(8,128)(2,1)} %g_hbm.1, s32[1]{0:T(128)} %bitcast.live_ref, bf16[1280,1024]{1,0:T(8,128)(2,1)} %get-tuple-element.46.att_ref.a_ref, ...), custom_call_target="tpu_custom_call" | custom-call | flops 2684354560 | bytes 28835840 | tf_op jit(solution)/shard_map/mid/pallas_call | solution.py:303
  78.3 81.5 %mlp.1 = (f32[1280,1024]{1,0:T(8,128)}, f32[1280,1024]{1,0:T(8,128)}, bf16[1024,4096]{1,0:T(8,128)(2,1)}, bf16[4096,1024]{1,0:T(8,128)(2,1)}) custom-call(bf16[1280,1024]{1,0:T(8,128)(2,1)} %get-tuple-element.49.nm_ref, bf16[1280,1024]{1,0:T(8,128)(2,1)} %get-tuple-element.50.gm_ref, bf16[1024,4096]{1,0:T(8,128)(2,1)} %wu_ref.1, bf16[4096,1024]{1,0:T(8,128)(2,1)} %wd_ref.1), custom_call_target="tpu_custom_call" | custom-call | flops 64424509440 | bytes 49283072 | tf_op jit(solution)/shard_map/mlp/pallas_call | solution.py:357
  159.9 17.6 %post.1 = (bf16[1,5,16,16,1024]{4,3,2,1,0:T(8,128)(2,1)}, f32[1280,1024]{1,0:T(8,128)}, bf16[1280,1024]{1,0:T(8,128)(2,1)}, bf16[1280,1024]{1,0:T(8,128)(2,1)}, f32[8,1024]{1,0:T(8,128)}) custom-call(s32[1]{0:T(128)} %bitcast.live_ref, f32[1280,1024]{1,0:T(8,128)} %get-tuple-element.48.mid_ref, f32[1280,1024]{1,0:T(8,128)} %get-tuple-element.51.mo_ref, ...), custom_call_target="tpu_custom_call" | custom-call | flops 2684354560 | bytes 39321600 | tf_op jit(solution)/shard_map/post/pallas_call | solution.py:436
  177.5 6.3 outer.7
  183.9 35.5 %attn_bwd_main.1 = (bf16[960,1024]{1,0:T(8,128)(2,1)}, bf16[960,1024]{1,0:T(8,128)(2,1)}, bf16[960,1024]{1,0:T(8,128)(2,1)}) custom-call(s32[1]{0:T(128)} %bitcast.1.ok_ref, bf16[1280,1024]{1,0:T(8,128)(2,1)} %get-tuple-element.41.q_ref, bf16[1280,1024]{1,0:T(8,128)(2,1)} %get-tuple-element.42.k_ref, bf16[1280,1024]{1,0:T(8,128)(2,1)} %get-tuple-element.43.v_ref, ...), custom_call_target="tpu_custom_call" | custom-call | flops 10485760000 | bytes 23592960 | tf_op jit(solution)/shard_map/attn_bwd_main/pallas_call | solution.py:235
  219.4 1.7 constant_dynamic-update-slice_fusion.1
  221.1 21.3 %attn_bwd_paired.1 = (bf16[320,1024]{1,0:T(8,128)(2,1)}, f32[320,1024]{1,0:T(8,128)}, f32[320,1024]{1,0:T(8,128)}, bf16[2,320,1024]{2,1,0:T(8,128)(2,1)}) custom-call(s32[1]{0:T(128)} %bitcast.1.ok_ref, bf16[1280,1024]{1,0:T(8,128)(2,1)} %get-tuple-element.41.q_ref, bf16[1280,1024]{1,0:T(8,128)(2,1)} %get-tuple-element.42.k_ref, ...), custom_call_target="tpu_custom_call" | custom-call | flops 4194304000 | bytes 15728640 | tf_op jit(solution)/shard_map/attn_bwd_paired/pallas_call | solution.py:256
  242.3 1.2 constant_dynamic-update-slice_fusion.dq_ref.b_ref
  243.5 1.5 copy-done.2
  245.0 6.3 outer.4
  251.5 30.4 %collective-permute-done.1 = bf16[2,320,1024]{2,1,0:T(8,128)(2,1)S(1)} collective-permute-done((bf16[2,320,1024]{2,1,0:T(8,128)(2,1)}, bf16[2,320,1024]{2,1,0:T(8,128)(2,1)S(1)}, u32[]{:S(2)}, u32[]{:S(2)}) %collective-permute-start.1) | collective-permute-done | bytes 1310752 | tf_op jit(solution)/shard_map/ppermute | solution.py:526
  282.9 0.9 copy-done.1
  283.8 1.8 pad_maximum_fusion.1.dv_ref.b_ref
  285.6 6.3 outer.6
  292.5 1.0 copy-done
  293.5 1.8 pad_maximum_fusion.dk_ref.b_ref
  295.3 6.3 outer.5
  302.5 18.1 %final.1 = (bf16[1,5,16,16,1024]{4,3,2,1,0:T(8,128)(2,1)}, f32[8,1024]{1,0:T(8,128)}) custom-call(bf16[1280,1024]{1,0:T(8,128)(2,1)} %copy-done.2, bf16[1280,1024]{1,0:T(8,128)(2,1)} %pad_maximum_fusion.dk_ref.b_ref, bf16[1280,1024]{1,0:T(8,128)(2,1)} %pad_maximum_fusion.1.dv_ref.b_ref, bf16[1024,1024]{1,0:T(8,128)(2,1)} %wq_ref.1, ...), custom_call_target="tpu_custom_call" | custom-call | flops 8053063680 | bytes 18350080 | tf_op jit(solution)/shard_map/final/pallas_call | solution.py:512
  320.6 0.8 slice.14
  321.7 1.8 collective-permute-start.6
  323.5 1.9 collective-permute-done.2
  326.6 0.9 collective-permute-done.6
  327.6 0.9 add_bitcast_fusion.2
  328.5 49.2 %reduce-scatter.11.cloned.1.call-done = bf16[64,1024]{1,0:T(8,128)(2,1)} async-done(((bf16[1024,1024]{1,0:T(8,128)(2,1)}), bf16[64,1024]{1,0:T(8,128)(2,1)}) %reduce-scatter.11.cloned.1.call-update) | async-done | bytes 131088 | tf_op jit(solution)/shard_map/reduce_scatter | solution.py:530
  377.7 1.5 collective-permute-start.5
  379.2 106.6 %reduce-scatter.17.cloned.1.call-done = bf16[256,1024]{1,0:T(8,128)(2,1)} async-done(((bf16[4096,1024]{1,0:T(8,128)(2,1)}), bf16[256,1024]{1,0:T(8,128)(2,1)}) %reduce-scatter.17.cloned.1.call-update) | async-done | bytes 524304 | tf_op jit(solution)/shard_map/reduce_scatter | solution.py:530
  485.8 1.5 collective-permute-start.8
  487.3 0.9 add_bitcast_fusion.5
  488.2 0.8 copy.24
  489.7 61.5 %reduce-scatter.9.cloned.1.call-done = bf16[64,1024]{1,0:T(8,128)(2,1)} async-done(((bf16[1024,1024]{1,0:T(8,128)(2,1)}), bf16[64,1024]{1,0:T(8,128)(2,1)}) %reduce-scatter.9.cloned.1.call-update) | async-done | bytes 131088 | tf_op jit(solution)/shard_map/reduce_scatter | solution.py:530
  551.2 1.5 collective-permute-start.4
  552.7 106.1 %reduce-scatter.15.cloned.1.call-done = bf16[64,4096]{1,0:T(8,128)(2,1)} async-done(((bf16[1024,4096]{1,0:T(8,128)(2,1)}), bf16[64,4096]{1,0:T(8,128)(2,1)}) %reduce-scatter.15.cloned.1.call-update) | async-done | bytes 524304 | tf_op jit(solution)/shard_map/reduce_scatter | solution.py:530
  658.7 1.5 collective-permute-start.7
  660.2 0.9 add_bitcast_fusion.3
  661.1 0.8 copy.23
  661.9 1.0 add_bitcast_fusion.4
  662.9 0.8 copy.22
  663.8 1.2 copy.26
  665.0 7.7 %collective-permute-done.7 = bf16[64,4096]{1,0:T(8,128)(2,1)S(1)} collective-permute-done((bf16[64,4096]{1,0:T(8,128)(2,1)}, bf16[64,4096]{1,0:T(8,128)(2,1)S(1)}, u32[]{:S(2)}, u32[]{:S(2)}) %collective-permute-start.7) | collective-permute-done | bytes 524320 | tf_op jit(solution)/shard_map/ppermute | solution.py:526
  672.8 1.2 copy.25
  (45 shorter events, 5.3 us)
Async XLA Ops:
  7.2 314.6 %reduce-scatter.13.cloned.1.call-start = ((), (), s32[]{:S(2)}) async-start(), calls=%async_computation.9 | async-start | bytes 2228224 | tf_op jit(solution)/shard_map/reduce_scatter | solution.py:530
  8.4 22.8 %collective-permute-start = (bf16[5,4,16,1024]{3,2,1,0:T(8,128)(2,1)S(1)}, bf16[5,4,16,1024]{3,2,1,0:T(8,128)(2,1)S(1)}, u32[]{:S(2)}, u32[]{:S(2)}) collective-permute-start(bf16[5,4,16,1024]{3,2,1,0:T(8,128)(2,1)S(1)} %dynamic-slice_bitcast_fusion), channel_id=1, source_target_pairs={{0,1},{1,0},{2,3},{3,2},{4,5},{5,4},{6,7},{7,6},{8,9},{9,8},{10,11... | collective-permute-start | bytes 1966088 | tf_op jit(solution)/shard_map/ppermute | solution.py:526
  31.2 0.8 copy-start.8
  183.8 142.2 %reduce-scatter.7.cloned.1.call-start = ((), (), s32[]{:S(2)}) async-start(), calls=%async_computation.6 | async-start | bytes 2228224 | tf_op jit(solution)/shard_map/reduce_scatter | solution.py:530
  243.5 1.5 copy-start.2
  251.3 30.9 %copy-start.3 = (f32[320,1024]{1,0:T(8,128)S(1)}, f32[320,1024]{1,0:T(8,128)}, u32[]{:S(2)}) copy-start(f32[320,1024]{1,0:T(8,128)} %get-tuple-element.61) | copy-start | bytes 3932164
  251.3 30.9 %copy-start.4 = (f32[320,1024]{1,0:T(8,128)S(1)}, f32[320,1024]{1,0:T(8,128)}, u32[]{:S(2)}) copy-start(f32[320,1024]{1,0:T(8,128)} %get-tuple-element.64) | copy-start | bytes 3932164
  251.3 126.4 %reduce-scatter.11.cloned.1.call-start = ((), (), s32[]{:S(2)}) async-start(), calls=%async_computation.8 | async-start | bytes 2228224 | tf_op jit(solution)/shard_map/reduce_scatter | solution.py:530
  251.4 30.5 %collective-permute-start.1 = (bf16[2,320,1024]{2,1,0:T(8,128)(2,1)}, bf16[2,320,1024]{2,1,0:T(8,128)(2,1)S(1)}, u32[]{:S(2)}, u32[]{:S(2)}) collective-permute-start(bf16[2,320,1024]{2,1,0:T(8,128)(2,1)} %get-tuple-element.62), channel_id=1, source_target_pairs={{0,1},{1,0},{2,3},{3,2},{4,5},{5,4},{6,7},{7,6},{8,9},{9,8},{10,11... | collective-permute-start | bytes 3932168 | tf_op jit(solution)/shard_map/ppermute | solution.py:526
  282.2 1.5 copy-start.1
  291.9 193.9 %reduce-scatter.17.cloned.1.call-start = ((), (), s32[]{:S(2)}) async-start(), calls=%async_computation.11 | async-start | bytes 8912896 | tf_op jit(solution)/shard_map/reduce_scatter | solution.py:530
  291.9 1.6 copy-start
  292.5 258.7 %reduce-scatter.9.cloned.1.call-start = ((), (), s32[]{:S(2)}) async-start(), calls=%async_computation.7 | async-start | bytes 2228224 | tf_op jit(solution)/shard_map/reduce_scatter | solution.py:530
  301.7 357.1 %reduce-scatter.15.cloned.1.call-start = ((), (), s32[]{:S(2)}) async-start(), calls=%async_computation.10 | async-start | bytes 8912896 | tf_op jit(solution)/shard_map/reduce_scatter | solution.py:530
  301.7 0.8 copy-start.7
  321.4 4.0 collective-permute-start.2
  321.7 5.8 collective-permute-start.6
  326.0 161.2 %collective-permute-start.3 = (bf16[64,1024]{1,0:T(8,128)(2,1)}, bf16[64,1024]{1,0:T(8,128)(2,1)S(1)}, u32[]{:S(2)}, u32[]{:S(2)}) collective-permute-start(bf16[64,1024]{1,0:T(8,128)(2,1)} %reduce-scatter.7.cloned.1.call-done), channel_id=1, source_target_pairs={{0,1},{1,0},{2,3},{3,2},{4,5},{5,4},{6,7},{7,6},{8,9},{9,8},{10,11... | collective-permute-start | bytes 393224 | tf_op jit(solution)/shard_map/ppermute | solution.py:526
  377.7 282.5 %collective-permute-start.5 = (bf16[64,1024]{1,0:T(8,128)(2,1)}, bf16[64,1024]{1,0:T(8,128)(2,1)S(1)}, u32[]{:S(2)}, u32[]{:S(2)}) collective-permute-start(bf16[64,1024]{1,0:T(8,128)(2,1)} %reduce-scatter.11.cloned.1.call-done), channel_id=1, source_target_pairs={{0,1},{1,0},{2,3},{3,2},{4,5},{5,4},{6,7},{7,6},{8,9},{9,8},{10,11... | collective-permute-start | bytes 393224 | tf_op jit(solution)/shard_map/ppermute | solution.py:526
  485.8 177.9 %copy-start.5 = (bf16[256,1024]{1,0:T(8,128)(2,1)S(1)}, bf16[256,1024]{1,0:T(8,128)(2,1)}, u32[]{:S(2)}) copy-start(bf16[256,1024]{1,0:T(8,128)(2,1)} %reduce-scatter.17.cloned.1.call-done) | copy-start | bytes 1572868
  485.8 177.9 %collective-permute-start.8 = (bf16[256,1024]{1,0:T(8,128)(2,1)}, bf16[256,1024]{1,0:T(8,128)(2,1)S(1)}, u32[]{:S(2)}, u32[]{:S(2)}) collective-permute-start(bf16[256,1024]{1,0:T(8,128)(2,1)} %reduce-scatter.17.cloned.1.call-done), channel_id=1, source_target_pairs={{0,1},{1,0},{2,3},{3,2},{4,5},{5,4},{6,7},{7,6},{8,9},{9,8},{10,11... | collective-permute-start | bytes 1572872 | tf_op jit(solution)/shard_map/ppermute | solution.py:526
  551.2 110.7 %collective-permute-start.4 = (bf16[64,1024]{1,0:T(8,128)(2,1)}, bf16[64,1024]{1,0:T(8,128)(2,1)S(1)}, u32[]{:S(2)}, u32[]{:S(2)}) collective-permute-start(bf16[64,1024]{1,0:T(8,128)(2,1)} %reduce-scatter.9.cloned.1.call-done), channel_id=1, source_target_pairs={{0,1},{1,0},{2,3},{3,2},{4,5},{5,4},{6,7},{7,6},{8,9},{9,8},{10,11... | collective-permute-start | bytes 393224 | tf_op jit(solution)/shard_map/ppermute | solution.py:526
  658.7 13.9 %collective-permute-start.7 = (bf16[64,4096]{1,0:T(8,128)(2,1)}, bf16[64,4096]{1,0:T(8,128)(2,1)S(1)}, u32[]{:S(2)}, u32[]{:S(2)}) collective-permute-start(bf16[64,4096]{1,0:T(8,128)(2,1)} %reduce-scatter.15.cloned.1.call-done), channel_id=1, source_target_pairs={{0,1},{1,0},{2,3},{3,2},{4,5},{5,4},{6,7},{7,6},{8,9},{9,8},{10,11... | collective-permute-start | bytes 1572872 | tf_op jit(solution)/shard_map/ppermute | solution.py:526
  661.9 10.8 %copy-start.6 = (bf16[64,4096]{1,0:T(8,128)(2,1)S(1)}, bf16[64,4096]{1,0:T(8,128)(2,1)}, u32[]{:S(2)}) copy-start(bf16[64,4096]{1,0:T(8,128)(2,1)} %reduce-scatter.15.cloned.1.call-done) | copy-start | bytes 1572868
Sparse Core Ops, SparseCore 0:
  184.0 61.9 reduce-scatter.12
  251.4 61.8 reduce-scatter.6
  317.1 60.5 reduce-scatter.10
  382.2 103.5 reduce-scatter.16
  489.8 61.3 reduce-scatter.8
  555.1 103.5 reduce-scatter.14

commit v2 on v1

--- a/solution.py
+++ b/solution.py
@@ -522,13 +522,230 @@
     )(dq, dk, dv, wq, wk, wv, xw, gmid, mod)
 
 
+LANES = 512
+
+
+class Reduce:
+    def __init__(self, dp, total_rows, orders, vmem_source):
+        self.bits = list(range(dp.bit_length() - 2, 0, -1))
+        self.nz = len(self.bits)
+        self.stages = self.nz + 1
+        self.depth = self.stages + 4
+        self.r = total_rows // dp
+        self.orders = orders
+        self.vmem_source = vmem_source
+        self.dp = dp
+
+    def scratch(self):
+        r, nz, k = self.r, self.nz, self.stages
+        cube = (2,) * nz
+        out = [] if self.vmem_source else [pltpu.VMEM(cube + (r, LANES), BF16)]
+        out += [pltpu.VMEM((2,) + cube + (r, LANES), BF16)]
+        for _ in range(2):
+            for i in range(k):
+                block = (2,) * (k - 1 - i) + (r, 128)
+                out += [pltpu.VMEM(block, BF16), pltpu.VMEM(block, BF16), pltpu.VMEM((2,) + block, BF16)]
+        out += [pltpu.VMEM((2, r, 128), BF16), pltpu.VMEM((2, 2, r, 128), BF16), pltpu.VMEM((r, LANES), F32)]
+        out += [pltpu.SemaphoreType.DMA((2 * k + 4,)), pltpu.SemaphoreType.DMA((2 * k + 2, 2))]
+        return out
+
+    def bind(self, refs, source, write):
+        refs = list(refs)
+        self.own = None if self.vmem_source else refs.pop(0)
+        self.got_core = refs.pop(0)
+        self.send, self.keep, self.got = {}, {}, {}
+        for p in range(2):
+            for i in range(self.stages):
+                self.send[p, i], self.keep[p, i], self.got[p, i] = refs.pop(0), refs.pop(0), refs.pop(0)
+        self.fin, self.got_fin, self.ostage, self.ssem, self.rsem = refs
+        self.source, self.write = source, write
+        self.me, self.band = lax.axis_index("dp"), lax.axis_index("band")
+
+    def place(self, axis):
+        return self.band if axis == 0 else lax.rem(self.me // (1 << axis), 2)
+
+    def partner(self, axis):
+        if axis == 0:
+            return (self.me, 1 - self.band)
+        bit = 1 if axis == -1 else 1 << axis
+        here = lax.rem(self.me // bit, 2)
+        return (self.me + bit - 2 * bit * here, self.band)
+
+    def barrier(self):
+        sem = pltpu.get_barrier_semaphore()
+        everyone = [-1, 0] + self.bits
+        for axis in everyone:
+            pl.semaphore_signal(sem, inc=1, device_id=self.partner(axis), device_id_type=pl.DeviceIdType.MESH)
+        pl.semaphore_wait(sem, len(everyone))
+
+    def remote(self, src, dst, s, slot, axis):
+        return pltpu.make_async_remote_copy(
+            src_ref=src,
+            dst_ref=dst,
+            send_sem=self.ssem.at[s],
+            recv_sem=self.rsem.at[s, slot],
+            device_id=self.partner(axis),
+            device_id_type=pl.DeviceIdType.MESH,
+        )
+
+    def core_copy(self, slot, src):
+        return self.remote(src, self.got_core.at[slot], 2 * self.stages, slot, -1)
+
+    def part_copy(self, p, i, slot):
+        return self.remote(self.send[p, i], self.got[p, i].at[slot], 2 * i + p, slot, self.orders[p][i])
+
+    def fin_copy(self, slot):
+        return self.remote(self.fin, self.got_fin.at[slot], 2 * self.stages + 1, slot, 0)
+
+    def pick(self, axes, axis, at):
+        return tuple(at if a == axis else slice(None) for a in axes)
+
+    def split_core(self, j, p):
+        slot = lax.rem(j, 2)
+        first = self.orders[p][0]
+        mine = self.place(first)
+        for dst, at in ((self.send[p, 0], 1 - mine), (self.keep[p, 0], mine)):
+            if first == 0:
+                lanes = pl.ds(pl.multiple_of((2 * p + at) * 128, 128), 128)
+                idx = (slice(None),) * (self.nz + 1) + (lanes,)
+                v = self.own_half(slot, idx) + self.got_core[(slot,) + idx].astype(F32)
+                dst[...] = v.astype(BF16)
+            else:
+                for b in range(2):
+                    lanes = slice((2 * p + b) * 128, (2 * p + b + 1) * 128)
+                    idx = self.pick(self.bits, first, at) + (slice(None), lanes)
+                    v = self.own_half(slot, idx) + self.got_core[(slot,) + idx].astype(F32)
+                    dst[(slice(None),) * (self.nz - 1) + (b,)] = v.astype(BF16)
+
+    def own_half(self, slot, idx):
+        if self.vmem_source:
+            return self.source(slot, idx).astype(F32)
+        return self.own[idx].astype(F32)
+
+    def split(self, j, p, i):
+        slot = lax.rem(j, 2)
+        axes = [a for a in self.bits + [0] if a not in self.orders[p][:i]]
+        axis = self.orders[p][i]
+        mine = self.place(axis)
+        for dst, at in ((self.send[p, i], 1 - mine), (self.keep[p, i], mine)):
+            idx = self.pick(axes, axis, at)
+            v = self.keep[p, i - 1][idx].astype(F32) + self.got[p, i - 1][(slot,) + idx].astype(F32)
+            dst[...] = v.astype(BF16)
+
+    def stage(self, s, j):
+        k = self.stages
+        slot = lax.rem(j, 2)
+        if s == 0:
+            if self.vmem_source:
+                self.core_copy(slot, self.source(slot, None)).start()
+            else:
+                self.source(j, self)
+        elif s == 1:
+            dummy = self.source(slot, None) if self.vmem_source else self.own
+            self.core_copy(slot, dummy).wait()
+            if not self.vmem_source:
+                pltpu.make_async_copy(self.own, self.own, self.ssem.at[2 * k + 2]).wait()
+            for p in range(2):
+                self.split_core(j, p)
+                self.part_copy(p, 0, slot).start()
+        elif s <= k:
+            for p in range(2):
+                self.part_copy(p, s - 2, slot).wait()
+                self.split(j, p, s - 1)
+                self.part_copy(p, s - 1, slot).start()
+        elif s == k + 1:
+            for p in range(2):
+                self.part_copy(p, k - 1, slot).wait()
+                v = self.keep[p, k - 1][...].astype(F32) + self.got[p, k - 1][slot].astype(F32)
+                self.fin[p] = v.astype(BF16)
+            self.fin_copy(slot).start()
+        elif s == k + 2:
+            self.fin_copy(slot).wait()
+            for p in range(2):
+                mine = pl.ds(pl.multiple_of((2 * p + self.band) * 128, 128), 128)
+                other = pl.ds(pl.multiple_of((2 * p + 1 - self.band) * 128, 128), 128)
+                self.ostage[:, mine] = self.fin[p].astype(F32)
+                self.ostage[:, other] = self.got_fin[slot, p].astype(F32)
+            self.write(j, self)
+        else:
+            pltpu.make_async_copy(self.ostage, self.ostage, self.ssem.at[2 * k + 3]).wait()
+
+    def tick(self, t, jobs):
+        for s in reversed(range(self.depth)):
+            j = t - s
+
+            @pl.when((j >= 0) & (j < jobs))
+            def _():
+                self.stage(s, j)
+
+
+def comm_kernel(sizes, red, *refs):
+    n = len(sizes)
+    srcs, outs, scratch = refs[:n], refs[n : 2 * n], refs[2 * n :]
+    core = lax.rem(lax.axis_index("dp"), 2)
+
+    def dispatch(j, body):
+        base = 0
+        for i, (q, wide) in enumerate(sizes):
+            count = q * wide
+
+            @pl.when((j >= base) & (j < base + count))
+            def _():
+                at = j - base
+                body(i, at // wide, pl.ds(pl.multiple_of(lax.rem(at, wide) * LANES, LANES), LANES))
+
+            base += count
+
+    def source(j, red):
+        def body(i, q, lanes):
+            cube = (slice(None),) * red.nz
+            pltpu.make_async_copy(srcs[i].at[cube + (core, q, slice(None), lanes)], red.own, red.ssem.at[2 * red.stages + 2]).start()
+            red.core_copy(lax.rem(j, 2), srcs[i].at[cube + (1 - core, q, slice(None), lanes)]).start()
+
+        dispatch(j, body)
+
+    def write(j, red):
+        def body(i, q, lanes):
+            pltpu.make_async_copy(red.ostage, outs[i].at[q, :, lanes], red.ssem.at[2 * red.stages + 3]).start()
+
+        dispatch(j, body)
+
+    red.bind(scratch, source, write)
+    red.barrier()
+    jobs = sum(q * wide for q, wide in sizes)
+
+    def body(t, _):
+        red.tick(t, jobs)
+        return 0
+
+    lax.fori_loop(0, jobs + red.depth - 1, body, 0)
+
+
+def reduce_all(grads):
+    dp = lax.axis_size("dp")
+    low = dp.bit_length() - 2
+    red = Reduce(dp, 1024, ((0, 1, *range(2, low + 1)), (1, 0, *range(2, low + 1))), False)
+    sizes, srcs, outs = [], [], []
+    for g in grads:
+        rows, cols = g.shape
+        q = rows // 1024
+        sizes.append((q, cols // LANES))
+        srcs.append(g.reshape((2,) * (red.nz + 1) + (q, red.r, cols)))
+        outs.append(jax.ShapeDtypeStruct((q, red.r, cols), F32))
+    sums = pl.pallas_call(
+        functools.partial(comm_kernel, sizes, red),
+        in_specs=[ANY] * len(srcs),
+        out_specs=[ANY] * len(srcs),
+        out_shape=outs,
+        scratch_shapes=red.scratch(),
+        compiler_params=params(collective_id=1, has_side_effects=True),
+        name="reduce_all",
+    )(*srcs)
+    return [s.reshape(-1) for s in sums]
+
+
 def band_swap(v):
     return lax.ppermute(v, "band", [(0, 1), (1, 0)])
-
-
-def reduced(grad):
-    share = lax.psum_scatter(grad, "dp", scatter_dimension=0, tiled=True)
-    return (share.astype(F32) + band_swap(share).astype(F32)).reshape(-1)
 
 
 def on_device(
@@ -550,19 +767,19 @@
     attended, lse = attn_fwd(halo_ok, q, k, v, kh, vh)
     ao, middle, nm, gw, gm = mid(cotangent, live, attended, w_out, xw, mod)
     mo, h, d_up, d_down = mlp(nm, gm, w_up, w_down)
-    g_up, g_down = reduced(d_up), reduced(d_down)
     block_output, gmid, ga, do, sums_m = post(live, middle, mo, h, gw, ao, mod, w_out, block_input)
-    g_out = reduced(outer(attended, ga))
+    d_out = outer(attended, ga)
     dq2, dk2, dv2, send = attn_bwd_paired(halo_ok, q, k, v, do, lse, kh, vh)
     got = band_swap(send).astype(F32)
     dq1, dk1, dv1 = attn_bwd_main(halo_ok, q, k, v, do, lse)
     dq = jnp.concatenate([dq1, dq2])
     dk = jnp.concatenate([dk1, (dk2 + got[0]).astype(BF16)])
     dv = jnp.concatenate([dv1, (dv2 + got[1]).astype(BF16)])
-    g_query, g_key, g_value = (reduced(outer(normed, d)) for d in (dq, dk, dv))
+    d_query, d_key, d_value = (outer(normed, d) for d in (dq, dk, dv))
     grad_input, sums_a = final(dq, dk, dv, w_query, w_key, w_value, xw, gmid, mod, block_input)
     mod_part = jnp.concatenate([sums_a[0:2], sums_m[0:4]])
     mod_total = mod_part + band_swap(mod_part)
+    g_up, g_down, g_out, g_query, g_key, g_value = reduce_all((d_up, d_down, d_out, d_query, d_key, d_value))
     return block_output, grad_input, mod_total[None], g_query, g_key, g_value, g_out, g_up, g_down
 
 

time: 682 us -> 462 us (0.68)
  waiting for transfers between devices: 365 us -> 0.01 us
  Pallas kernels: 261 us -> 429 us
  between operations: 16.3 us -> 2.76 us
    reduce_scatter x6 -> x0, waiting for transfers between devices: 323 us -> none  [reduced(): share = lax.psum_scatter(grad, 'dp', scatter_dimension=0, tiled=True)]
    pallas_call x0 -> x1, Pallas kernels: none -> 168 us  [reduce_all(): pl.pallas_call(functools.partial(comm_kernel, sizes, red), in_specs=[ANY]...]
    ppermute x9 -> x3, waiting for transfers between devices: 40.9 us -> 0.01 us  [band_swap(): return lax.ppermute(v, 'band', [(0, 1), (1, 0)])]
  transfers between devices with their start and end apart: 15 -> 3, of which waited for: 8 -> 0; matrix products, arithmetic and copies ran while one was open for 3% -> 3% of each run, Pallas kernels for 16% -> 52%
where the time goes in v2:
time: 462 us; the launch traced here: 461 us
  Pallas kernels  429 us (93%)
  local copies, waits for them, and re-layouts  20.8 us (5%)
  starting transfers between devices  5.14 us (1%)
    pallas_call x1, Pallas kernels, reduce_all(): pl.pallas_call(functools.partial(comm_kernel, sizes, red), in_specs=[ANY]...  168 us
    pallas_call x1, Pallas kernels, mlp(): pl.pallas_call(mlp_kernel, grid=(ff // tile,), in_specs=[whole((t, d)), w...  81.4 us
    pallas_call x1, Pallas kernels, attn_bwd_main(): pl.pallas_call(functools.partial(attn_bwd_kernel, 'main'), grid=(d // 128...  35.3 us
    pallas_call x1, Pallas kernels, attn_fwd(): pl.pallas_call(attn_fwd_kernel, grid=(d // 128,), in_specs=[pl.BlockSpec(...  28.5 us
    pallas_call x4, Pallas kernels, outer(): pl.pallas_call(outer_kernel, grid=(b.shape[1] // tile,), in_specs=[whole(...  26.1 us
    pallas_call x2, Pallas kernels, pre(): pl.pallas_call(functools.partial(pre_kernel, n_group, from_spots), grid=(...  21.9 us
    pallas_call x1, Pallas kernels, attn_bwd_paired(): pl.pallas_call(functools.partial(attn_bwd_kernel, 'paired'), grid=(d // 1...  21.3 us
    pallas_call x1, Pallas kernels, final(): pl.pallas_call(final_kernel, grid=(4,), in_specs=[blk, blk, blk, whole((d...  17.8 us
  transfers between devices with their start and end apart: 3, of which 0 were waited for; matrix products, arithmetic and copies ran while one was open for 3% of the time, Pallas kernels for 52%

profile of v2, /device:TPU:0, one launch (start us, length us, event | category | flops | bytes accessed | tf_op | source)
XLA Modules:
  0.0 461.2 jit_solution(1445894132576453092)
XLA Ops:
  0.6 1.1 dynamic-slice_bitcast_fusion
  1.8 3.0 collective-permute-start
  4.8 1.3 constant_dynamic-slice_fusion
  8.1 1.4 copy.28
  9.5 15.2 %pre.1 = (bf16[1280,1024]{1,0:T(8,128)(2,1)}, bf16[1280,1024]{1,0:T(8,128)(2,1)}, bf16[1280,1024]{1,0:T(8,128)(2,1)}, bf16[1280,1024]{1,0:T(8,128)(2,1)}, bf16[1280,1024]{1,0:T(8,128)(2,1)}) custom-call(bf16[1,5,16,16,1024]{4,3,2,1,0:T(8,128)(2,1)} %x_hbm.1, f32[6,1024]{1,0:T(8,128)} %bitcast.49, bf16[1024,1024]{1,0:T(8,128)(2,1)} %wq_ref.1, ...), custom_call_target="tpu_custom_call" | custom-call | flops 8053063680 | bytes 22020096 | tf_op jit(solution)/shard_map/pre/pallas_call | solution.py:108
  24.7 0.0 collective-permute-done.x_hbm
  24.7 0.0 copy-start.8
  24.7 0.8 copy-done.8
  25.5 6.7 %pre_halo.1 = (bf16[320,1024]{1,0:T(8,128)(2,1)}, bf16[320,1024]{1,0:T(8,128)(2,1)}) custom-call(bf16[5,4,16,1024]{3,2,1,0:T(8,128)(2,1)} %copy-done.8, f32[6,1024]{1,0:T(8,128)} %bitcast.50, bf16[1024,1024]{1,0:T(8,128)(2,1)} %wk_ref.1, bf16[1024,1024]{1,0:T(8,128)(2,1)} %wv_ref.1), custom_call_target="tpu_custom_call" | custom-call | flops 1342177280 | bytes 7471104 | tf_op jit(solution)/shard_map/pre_halo/pallas_call | solution.py:108
  32.2 28.5 %attn_fwd.1 = (bf16[1280,1024]{1,0:T(8,128)(2,1)}, f32[1280,1024]{1,0:T(8,128)}) custom-call(s32[1]{0:T(128)} %bitcast.1.ok_ref, bf16[1280,1024]{1,0:T(8,128)(2,1)} %get-tuple-element.47.q_ref, bf16[1280,1024]{1,0:T(8,128)(2,1)} %get-tuple-element.48.k_ref, bf16[1280,1024]{1,0:T(8,128)(2,1)} %get-tuple-element.49.v_ref, ...), custom_call_target="tpu_custom_call" | custom-call | flops 5872025600 | bytes 15728640 | tf_op jit(solution)/shard_map/attn_fwd/pallas_call | solution.py:171
  60.7 11.1 %mid.1 = (f32[1280,1024]{1,0:T(8,128)}, f32[1280,1024]{1,0:T(8,128)}, bf16[1280,1024]{1,0:T(8,128)(2,1)}, bf16[1280,1024]{1,0:T(8,128)(2,1)}, bf16[1280,1024]{1,0:T(8,128)(2,1)}) custom-call(bf16[1,5,16,16,1024]{4,3,2,1,0:T(8,128)(2,1)} %g_hbm.1, s32[1]{0:T(128)} %bitcast.live_ref, bf16[1280,1024]{1,0:T(8,128)(2,1)} %get-tuple-element.52.att_ref.a_ref, ...), custom_call_target="tpu_custom_call" | custom-call | flops 2684354560 | bytes 28835840 | tf_op jit(solution)/shard_map/mid/pallas_call | solution.py:303
  71.8 81.4 %mlp.1 = (f32[1280,1024]{1,0:T(8,128)}, f32[1280,1024]{1,0:T(8,128)}, bf16[1024,4096]{1,0:T(8,128)(2,1)}, bf16[4096,1024]{1,0:T(8,128)(2,1)}) custom-call(bf16[1280,1024]{1,0:T(8,128)(2,1)} %get-tuple-element.55.nm_ref, bf16[1280,1024]{1,0:T(8,128)(2,1)} %get-tuple-element.56.gm_ref, bf16[1024,4096]{1,0:T(8,128)(2,1)} %wu_ref.1, bf16[4096,1024]{1,0:T(8,128)(2,1)} %wd_ref.1), custom_call_target="tpu_custom_call" | custom-call | flops 64424509440 | bytes 49283072 | tf_op jit(solution)/shard_map/mlp/pallas_call | solution.py:357
  153.2 17.6 %post.1 = (bf16[1,5,16,16,1024]{4,3,2,1,0:T(8,128)(2,1)}, f32[1280,1024]{1,0:T(8,128)}, bf16[1280,1024]{1,0:T(8,128)(2,1)}, bf16[1280,1024]{1,0:T(8,128)(2,1)}, f32[8,1024]{1,0:T(8,128)}) custom-call(s32[1]{0:T(128)} %bitcast.live_ref, f32[1280,1024]{1,0:T(8,128)} %get-tuple-element.54.mid_ref, f32[1280,1024]{1,0:T(8,128)} %get-tuple-element.57.mo_ref, ...), custom_call_target="tpu_custom_call" | custom-call | flops 2684354560 | bytes 39321600 | tf_op jit(solution)/shard_map/post/pallas_call | solution.py:436
  170.9 0.8 slice.15
  171.6 21.3 %attn_bwd_paired.1 = (bf16[320,1024]{1,0:T(8,128)(2,1)}, f32[320,1024]{1,0:T(8,128)}, f32[320,1024]{1,0:T(8,128)}, bf16[2,320,1024]{2,1,0:T(8,128)(2,1)}) custom-call(s32[1]{0:T(128)} %bitcast.1.ok_ref, bf16[1280,1024]{1,0:T(8,128)(2,1)} %get-tuple-element.47.q_ref, bf16[1280,1024]{1,0:T(8,128)(2,1)} %get-tuple-element.48.k_ref, ...), custom_call_target="tpu_custom_call" | custom-call | flops 4194304000 | bytes 15728640 | tf_op jit(solution)/shard_map/attn_bwd_paired/pallas_call | solution.py:256
  192.9 0.1 collective-permute-start.1
  193.0 35.3 %attn_bwd_main.1 = (bf16[960,1024]{1,0:T(8,128)(2,1)}, bf16[960,1024]{1,0:T(8,128)(2,1)}, bf16[960,1024]{1,0:T(8,128)(2,1)}) custom-call(s32[1]{0:T(128)} %bitcast.1.ok_ref, bf16[1280,1024]{1,0:T(8,128)(2,1)} %get-tuple-element.47.q_ref, bf16[1280,1024]{1,0:T(8,128)(2,1)} %get-tuple-element.48.k_ref, bf16[1280,1024]{1,0:T(8,128)(2,1)} %get-tuple-element.49.v_ref, ...), custom_call_target="tpu_custom_call" | custom-call | flops 10485760000 | bytes 23592960 | tf_op jit(solution)/shard_map/attn_bwd_main/pallas_call | solution.py:235
  228.3 1.8 constant_dynamic-update-slice_fusion.1
  230.1 0.0 copy-done.7
  230.2 0.0 copy-start.2
  230.2 7.2 %outer.4 = bf16[1024,1024]{1,0:T(8,128)(2,1)} custom-call(bf16[1280,1024]{1,0:T(8,128)(2,1)} %get-tuple-element.52.att_ref.a_ref, bf16[1280,1024]{1,0:T(8,128)(2,1)} %get-tuple-element.77.b_ref), custom_call_target="tpu_custom_call" | custom-call | flops 2684354560 | bytes 7864320 | tf_op jit(solution)/shard_map/outer/pallas_call | solution.py:456
  237.4 0.0 copy-done.2
  237.4 6.3 %outer.5 = bf16[1024,1024]{1,0:T(8,128)(2,1)} custom-call(bf16[1280,1024]{1,0:T(8,128)(2,1)} %get-tuple-element.78.a_ref, bf16[1280,1024]{1,0:T(8,128)(2,1)} %copy-done.2), custom_call_target="tpu_custom_call" | custom-call | flops 2684354560 | bytes 7864320 | tf_op jit(solution)/shard_map/outer/pallas_call | solution.py:456
  243.7 0.0 collective-permute-done.1
  243.7 0.3 convert_element_type.23
  244.0 1.0 copy-done.3
  245.0 0.4 copy-done.4
  245.4 0.7 fusion.1
  246.1 0.9 copy-done
  247.0 0.6 copy-done.1
  247.6 2.7 pad_maximum_fusion
  250.2 6.3 %outer.7 = bf16[1024,1024]{1,0:T(8,128)(2,1)} custom-call(bf16[1280,1024]{1,0:T(8,128)(2,1)} %get-tuple-element.78.a_ref, bf16[1280,1024]{1,0:T(8,128)(2,1)} %get-tuple-element.99.dv_ref.b_ref), custom_call_target="tpu_custom_call" | custom-call | flops 2684354560 | bytes 7864320 | tf_op jit(solution)/shard_map/outer/pallas_call | solution.py:456
  256.5 17.8 %final.1 = (bf16[1,5,16,16,1024]{4,3,2,1,0:T(8,128)(2,1)}, f32[8,1024]{1,0:T(8,128)}) custom-call(bf16[1280,1024]{1,0:T(8,128)(2,1)} %copy-done.2, bf16[1280,1024]{1,0:T(8,128)(2,1)} %get-tuple-element.98.dk_ref.b_ref, bf16[1280,1024]{1,0:T(8,128)(2,1)} %get-tuple-element.99.dv_ref.b_ref, bf16[1024,1024]{1,0:T(8,128)(2,1)} %wq_ref.1, ...), custom_call_target="tpu_custom_call" | custom-call | flops 8053063680 | bytes 18350080 | tf_op jit(solution)/shard_map/final/pallas_call | solution.py:512
  274.3 0.8 slice.14
  275.1 2.0 collective-permute-start.2
  277.1 6.3 %outer.6 = bf16[1024,1024]{1,0:T(8,128)(2,1)} custom-call(bf16[1280,1024]{1,0:T(8,128)(2,1)} %get-tuple-element.78.a_ref, bf16[1280,1024]{1,0:T(8,128)(2,1)} %get-tuple-element.98.dk_ref.b_ref), custom_call_target="tpu_custom_call" | custom-call | flops 2684354560 | bytes 7864320 | tf_op jit(solution)/shard_map/outer/pallas_call | solution.py:456
  283.4 167.8 %reduce_all.1 = (f32[1,64,4096]{2,1,0:T(8,128)}, f32[4,64,1024]{2,1,0:T(8,128)}, f32[1,64,1024]{2,1,0:T(8,128)}, f32[1,64,1024]{2,1,0:T(8,128)}, f32[1,64,1024]{2,1,0:T(8,128)}, /*index=5*/f32[1,64,1024]{2,1,0:T(8,128)}) custom-call(bf16[2,2,2,2,1,64,4096]{6,5,4,3,2,1,0:T(8,128)(2,1)} %bitcast.39, bf16[2,2,2,2,4,64,1024]{6,5,4,3,2,1,0:T(8,128)(2,1)} %bitcast.40, ...), custom_call_target="tpu_custom_call" | custom-call | tf_op jit(solution)/shard_map/reduce_all/pallas_call | solution.py:735
  451.2 0.0 copy-start.6
  451.2 0.0 copy-start.5
  451.2 1.8 copy.21
  453.1 1.7 copy.22
  454.8 1.7 copy.23
  456.5 1.7 copy.24
  458.2 0.0 copy-done.6
  458.2 1.2 copy.25
  459.4 1.2 copy.26
  460.5 0.0 collective-permute-done.2
  460.5 0.6 copy.19
  (9 shorter events, 0.1 us)
Async XLA Ops:
  1.8 22.9 %collective-permute-start = (bf16[5,4,16,1024]{3,2,1,0:T(8,128)(2,1)S(1)}, bf16[5,4,16,1024]{3,2,1,0:T(8,128)(2,1)S(1)}, u32[]{:S(2)}, u32[]{:S(2)}) collective-permute-start(bf16[5,4,16,1024]{3,2,1,0:T(8,128)(2,1)S(1)} %dynamic-slice_bitcast_fusion), channel_id=1, source_target_pairs={{0,1},{1,0},{2,3},{3,2},{4,5},{5,4},{6,7},{7,6},{8,9},{9,8},{10,11... | collective-permute-start | bytes 1966088 | tf_op jit(solution)/shard_map/ppermute | solution.py:748
  24.7 0.8 copy-start.8
  192.9 50.8 %collective-permute-start.1 = (bf16[2,320,1024]{2,1,0:T(8,128)(2,1)}, bf16[2,320,1024]{2,1,0:T(8,128)(2,1)S(1)}, u32[]{:S(2)}, u32[]{:S(2)}) collective-permute-start(bf16[2,320,1024]{2,1,0:T(8,128)(2,1)} %get-tuple-element.68), channel_id=1, source_target_pairs={{0,1},{1,0},{2,3},{3,2},{4,5},{5,4},{6,7},{7,6},{8,9},{9,8},{10,11... | collective-permute-start | bytes 3932168 | tf_op jit(solution)/shard_map/ppermute | solution.py:748
  228.3 1.8 copy-start.7
  230.2 7.2 %copy-start.2 = (bf16[1280,1024]{1,0:T(8,128)(2,1)}, bf16[1280,1024]{1,0:T(8,128)(2,1)S(1)}, u32[]{:S(2)}) copy-start(bf16[1280,1024]{1,0:T(8,128)(2,1)S(1)} %constant_dynamic-update-slice_fusion.dq_ref.b_ref) | copy-start | bytes 7864324
  243.7 1.3 copy-start.3
  243.7 1.7 copy-start.4
  245.4 1.5 copy-start
  245.4 2.1 copy-start.1
  275.1 185.4 %collective-permute-start.2 = (f32[6,1024]{1,0:T(8,128)S(1)}, f32[6,1024]{1,0:T(8,128)S(1)}, u32[]{:S(2)}, u32[]{:S(2)}) collective-permute-start(f32[6,1024]{1,0:T(8,128)S(1)} %pad_maximum_fusion.2), channel_id=1, source_target_pairs={{0,1},{1,0},{2,3},{3,2},{4,5},{5,4},{6,7},{7,6},{8,9},{9,8},{10,11... | collective-permute-start | bytes 73736 | tf_op jit(solution)/shard_map/ppermute | solution.py:748
  451.2 7.0 %copy-start.6 = (f32[1,64,4096]{2,1,0:T(8,128)S(1)}, f32[1,64,4096]{2,1,0:T(8,128)}, u32[]{:S(2)}) copy-start(f32[1,64,4096]{2,1,0:T(8,128)} %get-tuple-element.83) | copy-start | bytes 3145732
  451.2 8.1 %copy-start.5 = (f32[4,64,1024]{2,1,0:T(8,128)S(1)}, f32[4,64,1024]{2,1,0:T(8,128)}, u32[]{:S(2)}) copy-start(f32[4,64,1024]{2,1,0:T(8,128)} %get-tuple-element.84) | copy-start | bytes 3145732

commit v3 on v1

v3 whole, which is shorter than its diff:
```python
import functools

import jax
import jax.numpy as jnp
from jax import lax
from jax.experimental import pallas as pl
from jax.experimental.pallas import tpu as pltpu
from jax.sharding import PartitionSpec as P

HEADS = 16
HEAD_DIM = 64
EPS = 1e-06
MASKED = -1e30
LOG2E = 1.4426950408889634
F32 = jnp.float32
BF16 = jnp.bfloat16
ANY = pl.BlockSpec(memory_space=pl.ANY)
VMEM_LIMIT = 60 * 1024 * 1024

MID_SPOTS = ((1, 0), (2, 0), (1, 1), (2, 1))


def group_spot(band, s):
    lone = 3 * band
    paired = 3 - 3 * band
    if s < 2:
        return lone, s
    if s < 6:
        return MID_SPOTS[s - 2]
    return paired, s - 6


def params(**kw):
    return pltpu.CompilerParams(vmem_limit_bytes=VMEM_LIMIT, **kw)


def dot(a, b, ca=1, cb=0):
    return lax.dot_general(a, b, (((ca,), (cb,)), ((), ())), preferred_element_type=F32)


def whole(shape):
    return pl.BlockSpec(shape, lambda *_: (0,) * len(shape), pipeline_mode=pl.Buffered(1))


def norm_stats(v):
    c = v - jnp.mean(v, axis=-1, keepdims=True)
    r = lax.rsqrt(jnp.mean(c * c, axis=-1, keepdims=True) + EPS)
    return c * r, r


def spot_copy(hbm, vmem, band, s, sem, out=False):
    g, j = group_spot(band, s)
    there = hbm.at[0, :, pl.ds(g * 4, 4), pl.ds(j * 8, 8), :]
    if out:
        return pltpu.make_async_copy(vmem.at[s], there, sem.at[s])
    return pltpu.make_async_copy(there, vmem.at[s], sem.at[s])


def pre_kernel(n_group, from_spots, x_hbm, mod_ref, *refs):
    n_mat = (len(refs) - 5) // 2 if from_spots else (len(refs) - 3) // 2
    w_refs = refs[:n_mat]
    outs = refs[n_mat:]
    if from_spots:
        xw_ref, normed_ref = outs[:2]
        o_refs = outs[2 : 2 + n_mat]
    else:
        o_refs = outs[:n_mat]
    stage, sem, nsc = outs[-3:] if not from_spots else outs[-3:]
    rows = nsc.shape[0] // n_group

    @pl.when(pl.program_id(0) == 0)
    def _():
        band = lax.axis_index("band")
        if from_spots:
            copies = [spot_copy(x_hbm, stage, band, s, sem) for s in range(n_group)]
        else:
            copies = [
                pltpu.make_async_copy(x_hbm.at[:, :, pl.ds(8 * s, 8), :], stage.at[s], sem.at[s])
                for s in range(n_group)
            ]
        for c in copies:
            c.start()
        for s in range(n_group):
            copies[s].wait()
            x = stage[s].astype(F32).reshape(rows, stage.shape[-1])
            n, _ = norm_stats(x)
            part = pl.ds(s * rows, rows)
            nsc[part, :] = (n * (1.0 + mod_ref[1:2, :]) + mod_ref[0:1, :]).astype(BF16)
            if from_spots:
                xw_ref[part, :] = x.astype(BF16)
                normed_ref[part, :] = nsc[part, :]

    for w_ref, o_ref in zip(w_refs, o_refs):
        o_ref[...] = dot(nsc[...], w_ref[...]).astype(BF16)


def pre(x, mod, weights, n_group, from_spots):
    d = x.shape[-1]
    frames = x.shape[1] if from_spots else x.shape[0]
    rows = frames * 32
    t = n_group * rows
    tile = 256
    o_tile = pl.BlockSpec((t, tile), lambda n: (0, n))
    full = pl.BlockSpec((t, d), lambda n: (0, 0))
    act = jax.ShapeDtypeStruct((t, d), BF16)
    k = len(weights)
    head = [act, act] if from_spots else []
    return pl.pallas_call(
        functools.partial(pre_kernel, n_group, from_spots),
        grid=(d // tile,),
        in_specs=[ANY, whole((6, d))] + [pl.BlockSpec((d, tile), lambda n: (0, n))] * k,
        out_specs=[full] * len(head) + [o_tile] * k,
        out_shape=head + [act] * k,
        scratch_shapes=[
            pltpu.VMEM((n_group, frames, 4, 8, d), BF16),
            pltpu.SemaphoreType.DMA((n_group,)),
            pltpu.VMEM((t, d), BF16),
        ],
        compiler_params=params(),
        name="pre" if from_spots else "pre_halo",
        cost_estimate=pl.CostEstimate(
            flops=2 * t * d * d * k, bytes_accessed=2 * (k * d * d + (k + 3) * t * d), transcendentals=0
        ),
    )(x, mod, *weights)


LANES = 512


class Reduce:
    def __init__(self, dp, total_rows, orders, vmem_source):
        self.bits = list(range(dp.bit_length() - 2, 0, -1))
        self.nz = len(self.bits)
        self.stages = self.nz + 1
        self.depth = self.stages + 4
        self.r = total_rows // dp
        self.orders = orders
        self.vmem_source = vmem_source
        self.dp = dp

    def scratch(self):
        r, nz, k = self.r, self.nz, self.stages
        cube = (2,) * nz
        out = [] if self.vmem_source else [pltpu.VMEM(cube + (r, LANES), BF16)]
        out += [pltpu.VMEM((2,) + cube + (r, LANES), BF16)]
        for _ in range(2):
            for i in range(k):
                block = (2,) * (k - 1 - i) + (r, 128)
                out += [pltpu.VMEM(block, BF16), pltpu.VMEM(block, BF16), pltpu.VMEM((2,) + block, BF16)]
        out += [pltpu.VMEM((2, r, 128), BF16), pltpu.VMEM((2, 2, r, 128), BF16), pltpu.VMEM((r, LANES), F32)]
        out += [pltpu.SemaphoreType.DMA((2 * k + 4,)), pltpu.SemaphoreType.DMA((2 * k + 2, 2))]
        return out

    def bind(self, refs, source, write):
        refs = list(refs)
        self.own = None if self.vmem_source else refs.pop(0)
        self.got_core = refs.pop(0)
        self.send, self.keep, self.got = {}, {}, {}
        for p in range(2):
            for i in range(self.stages):
                self.send[p, i], self.keep[p, i], self.got[p, i] = refs.pop(0), refs.pop(0), refs.pop(0)
        self.fin, self.got_fin, self.ostage, self.ssem, self.rsem = refs
        self.source, self.write = source, write
        self.me, self.band = lax.axis_index("dp"), lax.axis_index("band")

    def place(self, axis):
        return self.band if axis == 0 else lax.rem(self.me // (1 << axis), 2)

    def partner(self, axis):
        if axis == 0:
            return (self.me, 1 - self.band)
        bit = 1 if axis == -1 else 1 << axis
        here = lax.rem(self.me // bit, 2)
        return (self.me + bit - 2 * bit * here, self.band)

    def barrier(self):
        sem = pltpu.get_barrier_semaphore()
        everyone = [-1, 0] + self.bits
        for axis in everyone:
            pl.semaphore_signal(sem, inc=1, device_id=self.partner(axis), device_id_type=pl.DeviceIdType.MESH)
        pl.semaphore_wait(sem, len(everyone))

    def remote(self, src, dst, s, slot, axis):
        return pltpu.make_async_remote_copy(
            src_ref=src,
            dst_ref=dst,
            send_sem=self.ssem.at[s],
            recv_sem=self.rsem.at[s, slot],
            device_id=self.partner(axis),
            device_id_type=pl.DeviceIdType.MESH,
        )

    def core_copy(self, slot, src):
        return self.remote(src, self.got_core.at[slot], 2 * self.stages, slot, -1)

    def part_copy(self, p, i, slot):
        return self.remote(self.send[p, i], self.got[p, i].at[slot], 2 * i + p, slot, self.orders[p][i])

    def fin_copy(self, slot):
        return self.remote(self.fin, self.got_fin.at[slot], 2 * self.stages + 1, slot, 0)

    def pick(self, axes, axis, at):
        return tuple(at if a == axis else slice(None) for a in axes)

    def split_core(self, j, p):
        slot = lax.rem(j, 2)
        first = self.orders[p][0]
        mine = self.place(first)
        for dst, at in ((self.send[p, 0], 1 - mine), (self.keep[p, 0], mine)):
            if first == 0:
                lanes = pl.ds(pl.multiple_of((2 * p + at) * 128, 128), 128)
                idx = (slice(None),) * (self.nz + 1) + (lanes,)
                v = self.own_half(slot, idx) + self.got_core[(slot,) + idx].astype(F32)
                dst[...] = v.astype(BF16)
            else:
                for b in range(2):
                    lanes = slice((2 * p + b) * 128, (2 * p + b + 1) * 128)
                    idx = self.pick(self.bits, first, at) + (slice(None), lanes)
                    v = self.own_half(slot, idx) + self.got_core[(slot,) + idx].astype(F32)
                    dst[(slice(None),) * (self.nz - 1) + (b,)] = v.astype(BF16)

    def own_half(self, slot, idx):
        if self.vmem_source:
            return self.source(slot, idx).astype(F32)
        return self.own[idx].astype(F32)

    def split(self, j, p, i):
        slot = lax.rem(j, 2)
        axes = [a for a in self.bits + [0] if a not in self.orders[p][:i]]
        axis = self.orders[p][i]
        mine = self.place(axis)
        for dst, at in ((self.send[p, i], 1 - mine), (self.keep[p, i], mine)):
            idx = self.pick(axes, axis, at)
            v = self.keep[p, i - 1][idx].astype(F32) + self.got[p, i - 1][(slot,) + idx].astype(F32)
            dst[...] = v.astype(BF16)

    def stage(self, s, j):
        k = self.stages
        slot = lax.rem(j, 2)
        if s == 0:
            if self.vmem_source:
                self.core_copy(slot, self.source(slot, None)).start()
            else:
                self.source(j, self)
        elif s == 1:
            dummy = self.source(slot, None) if self.vmem_source else self.own
            self.core_copy(slot, dummy).wait()
            if not self.vmem_source:
                pltpu.make_async_copy(self.own, self.own, self.ssem.at[2 * k + 2]).wait()
            for p in range(2):
                self.split_core(j, p)
                self.part_copy(p, 0, slot).start()
        elif s <= k:
            for p in range(2):
                self.part_copy(p, s - 2, slot).wait()
                self.split(j, p, s - 1)
                self.part_copy(p, s - 1, slot).start()
        elif s == k + 1:
            for p in range(2):
                self.part_copy(p, k - 1, slot).wait()
                v = self.keep[p, k - 1][...].astype(F32) + self.got[p, k - 1][slot].astype(F32)
                self.fin[p] = v.astype(BF16)
            self.fin_copy(slot).start()
        elif s == k + 2:
            self.fin_copy(slot).wait()
            for p in range(2):
                mine = pl.ds(pl.multiple_of((2 * p + self.band) * 128, 128), 128)
                other = pl.ds(pl.multiple_of((2 * p + 1 - self.band) * 128, 128), 128)
                self.ostage[:, mine] = self.fin[p].astype(F32)
                self.ostage[:, other] = self.got_fin[slot, p].astype(F32)
            self.write(j, self)
        else:
            pltpu.make_async_copy(self.ostage, self.ostage, self.ssem.at[2 * k + 3]).wait()

    def tick(self, t, jobs):
        for s in reversed(range(self.depth)):
            j = t - s

            @pl.when((j >= 0) & (j < jobs))
            def _():
                self.stage(s, j)

    def plain(self, src, dst, send_sem, recv_sem, axis):
        return pltpu.make_async_remote_copy(
            src_ref=src,
            dst_ref=dst,
            send_sem=send_sem,
            recv_sem=recv_sem,
            device_id=self.partner(axis),
            device_id_type=pl.DeviceIdType.MESH,
        )

    def finish(self, t, jobs):
        def body(u, _):
            self.tick(u, jobs)
            return 0

        lax.fori_loop(t, jobs + self.depth - 1, body, 0)


def grad_arrays(red, grads):
    sizes, srcs, sums = [], [], []
    for g in grads:
        rows, cols = g.shape
        q = rows // (red.r * red.dp)
        sizes.append((q, cols // LANES))
        srcs.append(g.reshape((2,) * (red.nz + 1) + (q, red.r, cols)))
        sums.append(jax.ShapeDtypeStruct((q, red.r, cols), F32))
    return sizes, srcs, sums


def columns(i):
    return pl.ds(pl.multiple_of(i * LANES, LANES), LANES)


def bind_arrays(red, sizes, srcs, sums, scratch):
    def dispatch(j, body):
        base = 0
        for i, (q, wide) in enumerate(sizes):

            @pl.when((j >= base) & (j < base + q * wide))
            def _():
                at = j - base
                body(i, at // wide, columns(lax.rem(at, wide)))

            base += q * wide

    def source(j, red):
        core = lax.rem(red.me, 2)

        def body(i, q, lanes):
            cube = (slice(None),) * red.nz
            here = srcs[i].at[cube + (core, q, slice(None), lanes)]
            pltpu.make_async_copy(here, red.own, red.ssem.at[2 * red.stages + 2]).start()
            red.core_copy(lax.rem(j, 2), srcs[i].at[cube + (1 - core, q, slice(None), lanes)]).start()

        dispatch(j, body)

    def write(j, red):
        def body(i, q, lanes):
            pltpu.make_async_copy(red.ostage, sums[i].at[q, :, lanes], red.ssem.at[2 * red.stages + 3]).start()

        dispatch(j, body)

    red.bind(scratch, source, write)
    return sum(q * wide for q, wide in sizes)


def bind_tiles(red, tiles, write, scratch):
    core = lax.rem(lax.axis_index("dp"), 2)

    def source(slot, idx):
        if idx is None:
            return tiles.at[(slot,) + (slice(None),) * red.nz + (1 - core,)]
        return tiles[(slot,) + idx[: red.nz] + (core,) + idx[red.nz :]]

    red.bind(scratch, source, write)


def tile_scratch(red):
    return pltpu.VMEM((2,) + (2,) * (red.nz + 1) + (red.r, LANES), BF16)


def put_tile(red, tiles, slot, v):
    tiles[slot] = v.reshape((2,) * (red.nz + 1) + (red.r, LANES)).astype(BF16)


SCALE = HEAD_DIM**-0.5
SCALE2 = SCALE * LOG2E


def windows(r):
    return ((0, r), (r, r), (2 * r, 2 * r), (4 * r, 2 * r), (6 * r, r), (7 * r, r))


def head_masks(rows):
    left = lax.broadcasted_iota(jnp.int32, (rows, 128), 1) < 64
    return left, jnp.logical_not(left)


def only(mask, v):
    return jnp.where(mask, v, jnp.zeros_like(v))


def fill_shared(scratch, own_ref, halo_ref, r):
    for w in range(2):
        scratch[2 * r * w : 2 * r * w + r, :] = own_ref[(6 + w) * r : (7 + w) * r, :]
        scratch[2 * r * w + r : 2 * r * (w + 1), :] = halo_ref[r * w : r * (w + 1), :]


def attn_fwd_kernel(ok_ref, q_ref, k_ref, v_ref, kh_ref, vh_ref, o_ref, lse_ref, kc, vc):
    r = q_ref.shape[0] // 8
    fill_shared(kc, k_ref, kh_ref, r)
    fill_shared(vc, v_ref, vh_ref, r)
    col = lax.broadcasted_iota(jnp.int32, (1, 2 * r), 1)
    bias = jnp.where((col >= r) & (ok_ref[0] != 1), MASKED, 0.0)
    for w, (q0, qn) in enumerate(windows(r)):
        q = q_ref[q0 : q0 + qn, :]
        if w < 4:
            k, v = k_ref[q0 : q0 + qn, :], v_ref[q0 : q0 + qn, :]
        else:
            keys = slice(2 * r * (w - 4), 2 * r * (w - 3))
            k, v = kc[keys, :], vc[keys, :]
        masks = head_masks(qn)
        o, lse = [], []
        for mask in masks:
            s = dot(only(mask, q), k, 1, 1) * SCALE2
            if w >= 4:
                s = s + bias
            top = jnp.max(s, axis=-1, keepdims=True)
            e = jnp.exp2(s - top)
            total = jnp.sum(e, axis=-1, keepdims=True)
            o.append(dot(e.astype(BF16), v) * (1.0 / total))
            lse.append(top + jnp.log2(total))
        o_ref[q0 : q0 + qn, :] = jnp.where(masks[0], o[0], o[1]).astype(BF16)
        lse_ref[q0 : q0 + qn, :] = jnp.where(masks[0], lse[0], lse[1])


def attn_fwd(halo_ok, q, k, v, kh, vh):
    t, d = q.shape
    th = kh.shape[0]
    big = pl.BlockSpec((t, 128), lambda n: (0, n))
    small = pl.BlockSpec((th, 128), lambda n: (0, n))
    return pl.pallas_call(
        attn_fwd_kernel,
        grid=(d // 128,),
        in_specs=[pl.BlockSpec(memory_space=pltpu.SMEM), big, big, big, small, small],
        out_specs=[big, big],
        out_shape=[jax.ShapeDtypeStruct((t, d), BF16), jax.ShapeDtypeStruct((t, d), F32)],
        scratch_shapes=[pltpu.VMEM((2 * th, 128), BF16)] * 2,
        compiler_params=params(),
        name="attn_fwd",
        cost_estimate=pl.CostEstimate(flops=t * t * d, bytes_accessed=12 * t * d, transcendentals=t * t * 3),
    )(halo_ok, q, k, v, kh, vh)


def attn_bwd_kernel(n_red, sizes, red, ok_ref, q_ref, k_ref, v_ref, do_ref, lse_ref, kh_ref, vh_ref, *refs):
    srcs, (dq_ref, dk_ref, dv_ref), sums = refs[:n_red], refs[n_red : n_red + 3], refs[n_red + 3 : 2 * n_red + 3]
    kc, vc, own, hsend, hrecv, hsem, *scratch = refs[2 * n_red + 3 :]
    step, steps = pl.program_id(0), pl.num_programs(0)
    slot = lax.rem(step, 2)
    r = q_ref.shape[0] // 8
    jobs = bind_arrays(red, sizes, srcs, sums, scratch)

    @pl.when(step == 0)
    def _():
        red.barrier()

    fill_shared(kc, k_ref, kh_ref, r)
    fill_shared(vc, v_ref, vh_ref, r)
    row = lax.broadcasted_iota(jnp.int32, (2 * r, 1), 0)
    bias = jnp.where((row >= r) & (ok_ref[0] != 1), MASKED, 0.0)

    def window(w):
        q0, qn = windows(r)[w]
        rows = slice(q0, q0 + qn)
        q, do = q_ref[rows, :], do_ref[rows, :]
        if w < 4:
            k, v = k_ref[rows, :], v_ref[rows, :]
        else:
            keys = slice(2 * r * (w - 4), 2 * r * (w - 3))
            k, v = kc[keys, :], vc[keys, :]
        lse = jnp.transpose(lse_ref[rows, :])
        masks = head_masks(qn)
        dq, dk, dv = [], [], []
        for h, mask in enumerate(masks):
            s = dot(k, only(mask, q), 1, 1) * SCALE2
            if w >= 4:
                s = s + bias
            p = jnp.exp2(s - lse[64 * h : 64 * h + 1, :])
            dp = dot(v, only(mask, do), 1, 1)
            total = jnp.sum(p * dp, axis=0, keepdims=True)
            ds = (p * (dp - total)).astype(BF16)
            dv.append(dot(p.astype(BF16), do))
            dk.append(dot(ds, q))
            dq.append(dot(ds, k, 0, 0))
        dq_ref[rows, :] = (jnp.where(masks[0], dq[0], dq[1]) * SCALE).astype(BF16)
        left = head_masks(k.shape[0])[0]
        return rows, jnp.where(left, dk[0], dk[1]) * SCALE, jnp.where(left, dv[0], dv[1])

    red.tick(2 * step, jobs)
    for w in (4, 5):
        part = slice(r * (w - 4), r * (w - 3))
        for i, v in enumerate(window(w)[1:]):
            own[i, part, :] = v[:r, :]
            hsend[i, part, :] = v[r:, :].astype(BF16)
    swap = red.plain(hsend, hrecv.at[slot], hsem.at[0], hsem.at[1 + slot], 0)
    swap.start()
    red.tick(2 * step + 1, jobs)
    for w in range(4):
        rows, dk, dv = window(w)
        dk_ref[rows, :] = dk.astype(BF16)
        dv_ref[rows, :] = dv.astype(BF16)
    swap.wait()
    for i, ref in enumerate((dk_ref, dv_ref)):
        ref[6 * r :, :] = (own[i] + hrecv[slot, i].astype(F32)).astype(BF16)

    @pl.when(step == steps - 1)
    def _():
        red.finish(2 * steps, jobs)


def attn_bwd(halo_ok, q, k, v, do, lse, kh, vh, grads):
    t, d = q.shape
    th = kh.shape[0]
    big = pl.BlockSpec((t, 128), lambda n: (0, n))
    small = pl.BlockSpec((th, 128), lambda n: (0, n))
    low = lax.axis_size("dp").bit_length() - 2
    rest = tuple(range(3, low + 1))
    red = Reduce(lax.axis_size("dp"), 1024, ((1, 2, *rest, 0), (2, 1, *rest, 0)), False)
    sizes, srcs, sums = grad_arrays(red, grads)
    out = pl.pallas_call(
        functools.partial(attn_bwd_kernel, len(srcs), sizes, red),
        grid=(d // 128,),
        in_specs=[pl.BlockSpec(memory_space=pltpu.SMEM)] + [big] * 5 + [small] * 2 + [ANY] * len(srcs),
        out_specs=[big] * 3 + [ANY] * len(srcs),
        out_shape=[jax.ShapeDtypeStruct((t, d), BF16)] * 3 + sums,
        scratch_shapes=[
            pltpu.VMEM((2 * th, 128), BF16),
            pltpu.VMEM((2 * th, 128), BF16),
            pltpu.VMEM((2, th, 128), F32),
            pltpu.VMEM((2, th, 128), BF16),
            pltpu.VMEM((2, 2, th, 128), BF16),
            pltpu.SemaphoreType.DMA((3,)),
        ]
        + red.scratch(),
        compiler_params=params(collective_id=2, has_side_effects=True),
        name="attn_bwd",
        cost_estimate=pl.CostEstimate(flops=3 * t * t * d, bytes_accessed=18 * t * d, transcendentals=t * t * 3),
    )(halo_ok, q, k, v, do, lse, kh, vh, *srcs)
    return out[:3], [s.reshape(-1) for s in out[3:]]


def mid_kernel(g_hbm, live_ref, att_ref, w_ref, x_ref, mod_ref, ao_ref, mid_ref, nm_ref, gw_ref, gm_ref, stage, sem):
    step = pl.program_id(0)
    band = lax.axis_index("band")
    live = live_ref[0].astype(F32)
    n_group = stage.shape[0]
    per = n_group // 4
    rows = gw_ref.shape[0] // per

    @pl.when(step == 0)
    def _():
        for s in range(n_group):
            spot_copy(g_hbm, stage, band, s, sem).start()

    attn_out = dot(att_ref[...], w_ref[...])
    middle = x_ref[...].astype(F32) + (live * mod_ref[2:3, :]) * attn_out
    ao_ref[...] = attn_out
    mid_ref[...] = middle
    n, _ = norm_stats(middle)
    nm_ref[...] = (n * (1.0 + mod_ref[4:5, :]) + mod_ref[3:4, :]).astype(BF16)
    for i in range(per):
        s = step * per + i
        pltpu.make_async_copy(g_hbm.at[0, :, pl.ds(0, 4), pl.ds(0, 8), :], stage.at[s], sem.at[s]).wait()
        g = stage[s].astype(F32).reshape(rows, stage.shape[-1])
        part = pl.ds(i * rows, rows)
        gw_ref[part, :] = g.astype(BF16)
        gm_ref[part, :] = ((live * mod_ref[5:6, :]) * g).astype(BF16)


def mid(cot, live, attended, w_out, xw, mod):
    t, d = xw.shape
    frames = cot.shape[1]
    blk = pl.BlockSpec((t // 4, d), lambda m: (m, 0))
    bf, f32 = jax.ShapeDtypeStruct((t, d), BF16), jax.ShapeDtypeStruct((t, d), F32)
    return pl.pallas_call(
        mid_kernel,
        grid=(4,),
        in_specs=[ANY, pl.BlockSpec(memory_space=pltpu.SMEM), blk, whole((d, d)), blk, whole((6, d))],
        out_specs=[blk] * 5,
        out_shape=[f32, f32, bf, bf, bf],
        scratch_shapes=[pltpu.VMEM((8, frames, 4, 8, d), BF16), pltpu.SemaphoreType.DMA((8,))],
        compiler_params=params(),
        name="mid",
        cost_estimate=pl.CostEstimate(flops=2 * t * d * d, bytes_accessed=22 * t * d, transcendentals=0),
    )(cot, live, attended, w_out, xw, mod)


GELU_C = 0.7978845608
GELU_A = 0.044715


def col_sum(v):
    return jnp.sum(v, axis=0, keepdims=True)


def norm_back(h, n, r, gain):
    e = h * (1.0 + gain)
    return r * (e - jnp.mean(e, axis=-1, keepdims=True) - n * jnp.mean(e * n, axis=-1, keepdims=True))


def add_sums(ref, first, rows):
    sums = jnp.concatenate(rows + [jnp.zeros((ref.shape[0] - len(rows), ref.shape[1]), F32)], axis=0)

    @pl.when(first)
    def _():
        ref[...] = sums

    @pl.when(jnp.logical_not(first))
    def _():
        ref[...] += sums


def put_groups(out, stage, out_hbm, sem, block, blocks):
    band = lax.axis_index("band")
    n_group = stage.shape[0]
    per = n_group // blocks
    rows = out.shape[0] // per
    for k in range(blocks):

        @pl.when(block == k)
        def _():
            for i in range(per):
                s = k * per + i
                stage[s] = out[i * rows : (i + 1) * rows, :].reshape(stage.shape[1:]).astype(BF16)
                spot_copy(out_hbm, stage, band, s, sem, out=True).start()

    @pl.when(block == blocks - 1)
    def _():
        for s in range(n_group):
            spot_copy(out_hbm, stage, band, s, sem, out=True).wait()


def ff_kernel(
    n_ff, red, live_ref, nm_ref, gm_ref, wu_ref, wd_ref, mid_ref, g_ref, ao_ref, mod_ref, wo_ref,
    out_hbm, gmid_ref, ga_ref, do_ref, sums_ref, dwd_ref, gup_hbm,
    mo, h, hid, gp, nmt, tiles, stage, sem, *scratch,
):
    step, steps = pl.program_id(0), pl.num_programs(0)
    t = nm_ref.shape[0]
    chunk = t // 4

    def write(j, red):
        pltpu.make_async_copy(red.ostage, gup_hbm.at[:, columns(j)], red.ssem.at[2 * red.stages + 3]).start()

    bind_tiles(red, tiles, write, scratch)

    @pl.when(step == 0)
    def _():
        red.barrier()
        mo[...] = jnp.zeros_like(mo)
        h[...] = jnp.zeros_like(h)
        nmt[...] = jnp.transpose(nm_ref[...])

    red.tick(step - 1, n_ff)

    @pl.when(step < n_ff)
    def _():
        def rows(i, _):
            part = pl.ds(pl.multiple_of(i * chunk, chunk), chunk)
            v = dot(nm_ref[part, :], wu_ref[...])
            gh = dot(gm_ref[part, :], wd_ref[...], 1, 1)
            v2 = v * v
            th = jnp.tanh(v * (GELU_C + (GELU_C * GELU_A) * v2))
            half = 0.5 * th + 0.5
            hidden = (v * half).astype(BF16)
            slope = half + (0.5 * v) * (1.0 - th * th) * (GELU_C + (3.0 * GELU_C * GELU_A) * v2)
            gpre = (gh * slope).astype(BF16)
            hid[part, :] = hidden
            gp[part, :] = gpre
            mo[part, :] += dot(hidden, wd_ref[...])
            h[part, :] += dot(gpre, wu_ref[...], 1, 1)
            return 0

        lax.fori_loop(0, 4, rows, 0)
        put_tile(red, tiles, lax.rem(step, 2), dot(nmt[...], gp[...]))
        dwd_ref[...] = dot(hid[...], gm_ref[...], 0, 0).astype(BF16)

    @pl.when(step >= n_ff)
    def _():
        block = step - n_ff
        part = pl.ds(pl.multiple_of(block * chunk, chunk), chunk)
        live = live_ref[0].astype(F32)
        middle, g = mid_ref[...], g_ref[...].astype(F32)
        mlp_out, hh = mo[part, :], h[part, :]
        n, r = norm_stats(middle)
        gmid = g + norm_back(hh, n, r, mod_ref[4:5, :])
        gmid_ref[...] = gmid
        ga = ((live * mod_ref[2:3, :]) * gmid).astype(BF16)
        ga_ref[...] = ga
        do_ref[...] = dot(ga, wo_ref[...], 1, 1).astype(BF16)
        sums = [col_sum(live * ao_ref[...] * gmid), col_sum(hh), col_sum(hh * n), col_sum(live * mlp_out * g)]
        add_sums(sums_ref, block == 0, sums)
        put_groups(middle + (live * mod_ref[5:6, :]) * mlp_out, stage, out_hbm, sem, block, 4)

    @pl.when(step == steps - 1)
    def _():
        red.finish(steps - 1, n_ff)


def feed_forward(live, nm, gm, w_up, w_down, middle, gw, ao, mod, w_out, like):
    t, d = nm.shape
    ff = w_up.shape[1]
    n_ff = ff // LANES
    frames = like.shape[1]
    low = lax.axis_size("dp").bit_length() - 2
    rest = tuple(range(2, low + 1))
    red = Reduce(lax.axis_size("dp"), d, ((0, 1, *rest), (1, 0, *rest)), True)
    blk = pl.BlockSpec((t // 4, d), lambda i: (jnp.maximum(i - n_ff, 0), 0))
    up_tile = pl.BlockSpec((d, LANES), lambda i: (0, jnp.minimum(i, n_ff - 1)))
    down_tile = pl.BlockSpec((LANES, d), lambda i: (jnp.minimum(i, n_ff - 1), 0))
    bf, f32 = jax.ShapeDtypeStruct((t, d), BF16), jax.ShapeDtypeStruct((t, d), F32)
    return pl.pallas_call(
        functools.partial(ff_kernel, n_ff, red),
        grid=(n_ff + 4,),
        in_specs=[pl.BlockSpec(memory_space=pltpu.SMEM), whole((t, d)), whole((t, d)), up_tile, down_tile]
        + [blk, blk, blk, whole((6, d)), whole((d, d))],
        out_specs=[ANY, blk, blk, blk, pl.BlockSpec((8, d), lambda i: (0, 0)), down_tile, ANY],
        out_shape=[jax.ShapeDtypeStruct(like.shape, BF16), f32, bf, bf, jax.ShapeDtypeStruct((8, d), F32)]
        + [jax.ShapeDtypeStruct((ff, d), BF16), jax.ShapeDtypeStruct((red.r, ff), F32)],
        scratch_shapes=[
            pltpu.VMEM((t, d), F32),
            pltpu.VMEM((t, d), F32),
            pltpu.VMEM((t, LANES), BF16),
            pltpu.VMEM((t, LANES), BF16),
            pltpu.VMEM((d, t), BF16),
            tile_scratch(red),
            pltpu.VMEM((8, frames, 4, 8, d), BF16),
            pltpu.SemaphoreType.DMA((8,)),
        ]
        + red.scratch(),
        compiler_params=params(collective_id=1, has_side_effects=True),
        name="feed_forward",
        cost_estimate=pl.CostEstimate(flops=12 * t * d * ff, bytes_accessed=8 * d * ff + 12 * t * d, transcendentals=t * ff),
    )(live, nm, gm, w_up, w_down, middle, gw, ao, mod, w_out)


def outer_kernel(a_ref, b_ref, o_ref):
    o_ref[...] = dot(a_ref[...], b_ref[...], 0, 0).astype(BF16)


def outer(a, b):
    t, d = a.shape
    tile = 512
    return pl.pallas_call(
        outer_kernel,
        grid=(b.shape[1] // tile,),
        in_specs=[whole((t, d)), pl.BlockSpec((t, tile), lambda n: (0, n))],
        out_specs=pl.BlockSpec((d, tile), lambda n: (0, n)),
        out_shape=jax.ShapeDtypeStruct((d, b.shape[1]), BF16),
        compiler_params=params(),
        name="outer",
        cost_estimate=pl.CostEstimate(flops=2 * t * d * b.shape[1], bytes_accessed=6 * t * d, transcendentals=0),
    )(a, b)


def final_kernel(
    n_outer, red, nd_ref, *refs
):
    cols, rows = refs[:3], refs[3:6]
    wq_ref, wk_ref, wv_ref, x_ref, gmid_ref, mod_ref, out_hbm, sums_ref, gq_hbm, gk_hbm, gv_hbm = refs[6:17]
    ndt, tiles, stage, sem, *scratch = refs[17:]
    step, steps = pl.program_id(0), pl.num_programs(0)
    per = n_outer // 3

    def write(j, red):
        for i, ref in enumerate((gq_hbm, gk_hbm, gv_hbm)):

            @pl.when(j // per == i)
            def _():
                pltpu.make_async_copy(red.ostage, ref.at[:, columns(lax.rem(j, per))], red.ssem.at[2 * red.stages + 3]).start()

    bind_tiles(red, tiles, write, scratch)

    @pl.when(step == 0)
    def _():
        red.barrier()
        ndt[...] = jnp.transpose(nd_ref[...])

    red.tick(step - 1, n_outer)
    for i in range(3):

        @pl.when(step // per == i)
        def _():
            put_tile(red, tiles, lax.rem(step, 2), dot(ndt[...], cols[i][...]))

    @pl.when(step >= n_outer)
    def _():
        dq, dk, dv = (ref[...] for ref in rows)
        h = dot(dq, wq_ref[...], 1, 1) + dot(dk, wk_ref[...], 1, 1) + dot(dv, wv_ref[...], 1, 1)
        n, r = norm_stats(x_ref[...].astype(F32))
        add_sums(sums_ref, step == n_outer, [col_sum(h), col_sum(h * n)])
        put_groups(gmid_ref[...] + norm_back(h, n, r, mod_ref[1:2, :]), stage, out_hbm, sem, step - n_outer, 4)

    @pl.when(step == steps - 1)
    def _():
        red.finish(steps - 1, n_outer)


def final(normed, dq, dk, dv, wq, wk, wv, xw, gmid, mod, like):
    t, d = xw.shape
    frames = like.shape[1]
    per = d // LANES
    n_outer = 3 * per
    low = lax.axis_size("dp").bit_length() - 2
    rest = tuple(range(2, low + 1))
    red = Reduce(lax.axis_size("dp"), d, ((0, 1, *rest), (1, 0, *rest)), True)

    def col_spec(i):
        return pl.BlockSpec((t, LANES), lambda n: (0, jnp.clip(n - i * per, 0, per - 1)))

    blk = pl.BlockSpec((t // 4, d), lambda n: (jnp.maximum(n - n_outer, 0), 0))
    out = pl.pallas_call(
        functools.partial(final_kernel, n_outer, red),
        grid=(n_outer + 4,),
        in_specs=[whole((t, d))] + [col_spec(i) for i in range(3)] + [blk] * 3 + [whole((d, d))] * 3 + [blk, blk, whole((6, d))],
        out_specs=[ANY, pl.BlockSpec((8, d), lambda n: (0, 0))] + [ANY] * 3,
        out_shape=[jax.ShapeDtypeStruct(like.shape, BF16), jax.ShapeDtypeStruct((8, d), F32)]
        + [jax.ShapeDtypeStruct((red.r, d), F32)] * 3,
        scratch_shapes=[
            pltpu.VMEM((d, t), BF16),
            tile_scratch(red),
            pltpu.VMEM((8, frames, 4, 8, d), BF16),
            pltpu.SemaphoreType.DMA((8,)),
        ]
        + red.scratch(),
        compiler_params=params(collective_id=3, has_side_effects=True),
        name="final",
        cost_estimate=pl.CostEstimate(flops=12 * t * d * d, bytes_accessed=14 * t * d, transcendentals=0),
    )(normed, dq, dk, dv, dq, dk, dv, wq, wk, wv, xw, gmid, mod)
    return out[0], out[1], [g.reshape(-1) for g in out[2:]]


def band_swap(v):
    return lax.ppermute(v, "band", [(0, 1), (1, 0)])


def on_device(
    block_input, modulation, band_live, w_query, w_key, w_value, w_out, w_up, w_down, cotangent
):
    assert lax.axis_size("band") == 2 and block_input.shape[2:4] == (16, 16)
    band = lax.axis_index("band")
    flags = band_live[0]
    live_own = lax.dynamic_index_in_dim(flags, band, keepdims=True)
    live_other = lax.dynamic_index_in_dim(flags, 1 - band, keepdims=True)
    live = (live_own == 1).astype(jnp.int32)
    halo_ok = ((live_other == 1) | (live_own != 1)).astype(jnp.int32)
    mod = modulation[0]

    edge = lax.dynamic_slice_in_dim(block_input[0], 12 - 12 * band, 4, axis=1)
    x_halo = band_swap(edge)
    xw, normed, q, k, v = pre(block_input, mod, (w_query, w_key, w_value), 8, True)
    kh, vh = pre(x_halo, mod, (w_key, w_value), 2, False)
    attended, lse = attn_fwd(halo_ok, q, k, v, kh, vh)
    ao, middle, nm, gw, gm = mid(cotangent, live, attended, w_out, xw, mod)
    block_output, gmid, ga, do, sums_m, d_down, g_up = feed_forward(
        live, nm, gm, w_up, w_down, middle, gw, ao, mod, w_out, block_input
    )
    d_out = outer(attended, ga)
    (dq, dk, dv), (g_down, g_out) = attn_bwd(halo_ok, q, k, v, do, lse, kh, vh, (d_down, d_out))
    grad_input, sums_a, (g_query, g_key, g_value) = final(
        normed, dq, dk, dv, w_query, w_key, w_value, xw, gmid, mod, block_input
    )
    mod_part = jnp.concatenate([sums_a[0:2], sums_m[0:4]])
    mod_total = mod_part + band_swap(mod_part)
    return block_output, grad_input, mod_total[None], g_query, g_key, g_value, g_out, g_up.reshape(-1), g_down


def solution(mesh):
    return jax.shard_map(
        on_device,
        mesh=mesh,
        in_specs=(
            P("dp", None, "band", None, None),
            P("dp", None, None),
            P("dp", None),
            P(),
            P(),
            P(),
            P(),
            P(),
            P(),
            P("dp", None, "band", None, None),
        ),
        out_specs=(
            P("dp", None, "band", None, None),
            P("dp", None, "band", None, None),
            P("dp", None, None),
            P("dp"),
            P("dp"),
            P("dp"),
            P("dp"),
            P("dp"),
            P("dp"),
        ),
        check_vma=False,
    )
```

time: 682 us -> 357 us (0.52)
  waiting for transfers between devices: 365 us -> 0.01 us
  Pallas kernels: 261 us -> 331 us
  between operations: 16.3 us -> 2.73 us
  other arithmetic: 8.69 us -> 0.02 us
  starting transfers between devices: 11.9 us -> 4.55 us
    reduce_scatter x6 -> x0, waiting for transfers between devices: 323 us -> none  [reduced(): share = lax.psum_scatter(grad, 'dp', scatter_dimension=0, tiled=True)]
    pallas_call x5 -> x3, Pallas kernels: 174 us -> 264 us  [the longest x1 116 us: feed_forward(): pl.pallas_call(functools.partial(ff_kernel, n_ff, red), grid=(n_ff + 4,),...]
    ppermute x9 -> x2, waiting for transfers between devices: 40.9 us -> 0.01 us  [band_swap(): return lax.ppermute(v, 'band', [(0, 1), (1, 0)])]
    pallas_call x4 -> x1, Pallas kernels: 25.3 us -> 6.28 us  [outer(): pl.pallas_call(outer_kernel, grid=(b.shape[1] // tile,), in_specs=[whole(...]
    ppermute x9 -> x2, starting transfers between devices: 11.7 us -> 4.55 us  [band_swap(): return lax.ppermute(v, 'band', [(0, 1), (1, 0)])]
    unnamed x27 -> x24, local copies, waits for them, and re-layouts: 13.5 us -> 15.3 us
  transfers between devices with their start and end apart: 15 -> 2, of which waited for: 8 -> 0; matrix products, arithmetic and copies ran while one was open for 3% -> 3% of each run, Pallas kernels for 16% -> 4%
where the time goes in v3:
time: 357 us
  Pallas kernels  331 us (93%)
  local copies, waits for them, and re-layouts  18.7 us (5%)
  starting transfers between devices  4.55 us (1%)
    pallas_call x1, Pallas kernels, feed_forward(): pl.pallas_call(functools.partial(ff_kernel, n_ff, red), grid=(n_ff + 4,),...  116 us
    pallas_call x1, Pallas kernels, attn_bwd(): pl.pallas_call(functools.partial(attn_bwd_kernel, len(srcs), sizes, red),...  87.2 us
    pallas_call x1, Pallas kernels, final(): pl.pallas_call(functools.partial(final_kernel, n_outer, red), grid=(n_out...  60.6 us
    pallas_call x1, Pallas kernels, attn_fwd(): pl.pallas_call(attn_fwd_kernel, grid=(d // 128,), in_specs=[pl.BlockSpec(...  27.1 us
    pallas_call x2, Pallas kernels, pre(): pl.pallas_call(functools.partial(pre_kernel, n_group, from_spots), grid=(...  21.8 us
    unnamed x24, local copies, waits for them, and re-layouts  15.3 us
    pallas_call x1, Pallas kernels, mid(): pl.pallas_call(mid_kernel, grid=(4,), in_specs=[ANY, pl.BlockSpec(memory_...  11.2 us
  transfers between devices with their start and end apart: 2, of which 0 were waited for; matrix products, arithmetic and copies ran while one was open for 3% of the time, Pallas kernels for 4%

profile of v3, /device:TPU:0, one launch (start us, length us, event | category | flops | bytes accessed | tf_op | source)
XLA Modules:
  0.0 356.5 jit_solution(16431512629847303079)
XLA Ops:
  0.6 1.1 dynamic-slice_bitcast_fusion
  1.8 3.0 collective-permute-start
  4.8 1.3 constant_dynamic-slice_fusion
  8.1 1.4 copy.28
  9.5 15.2 %pre.1 = (bf16[1280,1024]{1,0:T(8,128)(2,1)}, bf16[1280,1024]{1,0:T(8,128)(2,1)}, bf16[1280,1024]{1,0:T(8,128)(2,1)}, bf16[1280,1024]{1,0:T(8,128)(2,1)}, bf16[1280,1024]{1,0:T(8,128)(2,1)}) custom-call(bf16[1,5,16,16,1024]{4,3,2,1,0:T(8,128)(2,1)} %x_hbm.1, f32[6,1024]{1,0:T(8,128)} %bitcast.37, bf16[1024,1024]{1,0:T(8,128)(2,1)} %refs_6_.1, ...), custom_call_target="tpu_custom_call" | custom-call | flops 8053063680 | bytes 22020096 | tf_op jit(solution)/shard_map/pre/pallas_call | solution.py:108
  24.6 0.0 collective-permute-done.x_hbm
  24.6 0.0 copy-start.6
  24.6 0.8 copy-done.6
  25.5 6.7 %pre_halo.1 = (bf16[320,1024]{1,0:T(8,128)(2,1)}, bf16[320,1024]{1,0:T(8,128)(2,1)}) custom-call(bf16[5,4,16,1024]{3,2,1,0:T(8,128)(2,1)} %copy-done.6, f32[6,1024]{1,0:T(8,128)} %bitcast.38, bf16[1024,1024]{1,0:T(8,128)(2,1)} %refs_7_.1, bf16[1024,1024]{1,0:T(8,128)(2,1)} %refs_8_.1), custom_call_target="tpu_custom_call" | custom-call | flops 1342177280 | bytes 7471104 | tf_op jit(solution)/shard_map/pre_halo/pallas_call | solution.py:108
  32.2 27.1 %attn_fwd.1 = (bf16[1280,1024]{1,0:T(8,128)(2,1)}, f32[1280,1024]{1,0:T(8,128)}) custom-call(s32[1]{0:T(128)} %bitcast.1.ok_ref, bf16[1280,1024]{1,0:T(8,128)(2,1)} %get-tuple-element.40.q_ref, bf16[1280,1024]{1,0:T(8,128)(2,1)} %get-tuple-element.41.k_ref, bf16[1280,1024]{1,0:T(8,128)(2,1)} %get-tuple-element.42.v_ref, ...), custom_call_target="tpu_custom_call" | custom-call | flops 1677721600 | bytes 15728640 | tf_op jit(solution)/shard_map/attn_fwd/pallas_call | solution.py:424
  59.2 11.2 %mid.1 = (f32[1280,1024]{1,0:T(8,128)}, f32[1280,1024]{1,0:T(8,128)}, bf16[1280,1024]{1,0:T(8,128)(2,1)}, bf16[1280,1024]{1,0:T(8,128)(2,1)}, bf16[1280,1024]{1,0:T(8,128)(2,1)}) custom-call(bf16[1,5,16,16,1024]{4,3,2,1,0:T(8,128)(2,1)} %g_hbm.1, s32[1]{0:T(128)} %bitcast.live_ref, bf16[1280,1024]{1,0:T(8,128)(2,1)} %get-tuple-element.45.att_ref.a_ref, ...), custom_call_target="tpu_custom_call" | custom-call | flops 2684354560 | bytes 28835840 | tf_op jit(solution)/shard_map/mid/pallas_call | solution.py:567
  70.5 116.3 %feed_forward.1 = (bf16[1,5,16,16,1024]{4,3,2,1,0:T(8,128)(2,1)}, f32[1280,1024]{1,0:T(8,128)}, bf16[1280,1024]{1,0:T(8,128)(2,1)}, bf16[1280,1024]{1,0:T(8,128)...) custom-call(s32[1]{0:T(128)} %bitcast.live_ref, ...), custom_call_target="tpu_custom_call" | custom-call | flops 64424509440 | bytes 49283072 | tf_op jit(solution)/shard_map/feed_forward/pallas_call | solution.py:704
  186.8 6.3 %outer.1 = bf16[1024,1024]{1,0:T(8,128)(2,1)} custom-call(bf16[1280,1024]{1,0:T(8,128)(2,1)} %get-tuple-element.45.att_ref.a_ref, bf16[1280,1024]{1,0:T(8,128)(2,1)} %get-tuple-element.57.b_ref), custom_call_target="tpu_custom_call" | custom-call | flops 2684354560 | bytes 7864320 | tf_op jit(solution)/shard_map/outer/pallas_call | solution.py:736
  193.1 87.2 %attn_bwd.1 = (bf16[1280,1024]{1,0:T(8,128)(2,1)}, bf16[1280,1024]{1,0:T(8,128)(2,1)}, bf16[1280,1024]{1,0:T(8,128)(2,1)}, f32[4,64,1024]{2,1,0:T(8,128)}, f32[1,64,1024]{2,1,0:T(8,128)}) custom-call(s32[1]{0:T(128)} %bitcast.1.ok_ref, bf16[1280,1024]{1,0:T(8,128)(2,1)} %get-tuple-element.40.q_ref, bf16[1280,1024]{1,0:T(8,128)(2,1)} %get-tuple-element.41.k_ref, ...), custom_call_target="tpu_custom_call" | custom-call | flops 5033164800 | bytes 23592960 | tf_op jit(solution)/shard_map/attn_bwd/pallas_call | solution.py:512
  280.2 0.0 copy-start.5
  280.3 0.0 copy-start.4
  280.3 60.6 %final.1 = (bf16[1,5,16,16,1024]{4,3,2,1,0:T(8,128)(2,1)}, f32[8,1024]{1,0:T(8,128)}, f32[64,1024]{1,0:T(8,128)}, f32[64,1024]{1,0:T(8,128)}, f32[64,1024]{1,0:T(8,128)}) custom-call(bf16[1280,1024]{1,0:T(8,128)(2,1)} %get-tuple-element.53.nd_ref, bf16[1280,1024]{1,0:T(8,128)(2,1)} %get-tuple-element.58.refs_0_.refs_3_, ...), custom_call_target="tpu_custom_call" | custom-call | flops 16106127360 | bytes 18350080 | tf_op jit(solution)/shard_map/final/pallas_call | solution.py:804
  340.9 0.0 copy-start.3
  340.9 0.0 copy-start.2
  340.9 0.9 slice.6
  341.8 0.0 copy-done.5
  341.8 1.5 collective-permute-start.1
  343.4 1.7 copy.21
  345.1 1.7 copy.22
  346.8 0.0 copy-start
  346.8 1.9 copy.23
  348.6 0.0 copy-done.4
  348.6 0.8 copy.24
  349.4 0.0 copy-done.3
  349.4 1.2 copy.26
  350.5 0.0 copy-done.2
  350.5 1.2 copy.25
  351.7 0.0 collective-permute-done.1
  351.7 0.6 copy.19
  352.4 0.0 copy-done
  352.4 0.0 copy-start.1
  352.4 1.5 copy.31
  353.8 1.2 copy-done.1
  355.0 1.5 copy.32
  (3 shorter events, 0.0 us)
Async XLA Ops:
  1.8 22.8 %collective-permute-start = (bf16[5,4,16,1024]{3,2,1,0:T(8,128)(2,1)S(1)}, bf16[5,4,16,1024]{3,2,1,0:T(8,128)(2,1)S(1)}, u32[]{:S(2)}, u32[]{:S(2)}) collective-permute-start(bf16[5,4,16,1024]{3,2,1,0:T(8,128)(2,1)S(1)} %dynamic-slice_bitcast_fusion), channel_id=1, source_target_pairs={{0,1},{1,0},{2,3},{3,2},{4,5},{5,4},{6,7},{7,6},{8,9},{9,8},{10,11... | collective-permute-start | bytes 1966088 | tf_op jit(solution)/shard_map/ppermute | solution.py:826
  24.6 0.8 copy-start.6
  280.2 61.6 %copy-start.5 = (f32[8,1024]{1,0:T(8,128)S(1)}, f32[8,1024]{1,0:T(8,128)}, u32[]{:S(2)}) copy-start(f32[8,1024]{1,0:T(8,128)} %get-tuple-element.64) | copy-start | bytes 98308
  280.3 68.4 %copy-start.4 = (f32[1,64,1024]{2,1,0:T(8,128)S(1)}, f32[1,64,1024]{2,1,0:T(8,128)}, u32[]{:S(2)}) copy-start(f32[1,64,1024]{2,1,0:T(8,128)} %get-tuple-element.68) | copy-start | bytes 786436
  340.9 8.5 %copy-start.3 = (f32[4,64,1024]{2,1,0:T(8,128)S(1)}, f32[4,64,1024]{2,1,0:T(8,128)}, u32[]{:S(2)}) copy-start(f32[4,64,1024]{2,1,0:T(8,128)} %get-tuple-element.70) | copy-start | bytes 3145732
  340.9 9.6 %copy-start.2 = (f32[64,4096]{1,0:T(8,128)S(1)}, f32[64,4096]{1,0:T(8,128)}, u32[]{:S(2)}) copy-start(f32[64,4096]{1,0:T(8,128)} %get-tuple-element.69) | copy-start | bytes 3145732
  341.8 9.9 %collective-permute-start.1 = (f32[6,1024]{1,0:T(8,128)S(1)}, f32[6,1024]{1,0:T(8,128)S(1)}, u32[]{:S(2)}, u32[]{:S(2)}) collective-permute-start(f32[6,1024]{1,0:T(8,128)S(1)} %pad_maximum_fusion), channel_id=1, source_target_pairs={{0,1},{1,0},{2,3},{3,2},{4,5},{5,4},{6,7},{7,6},{8,9},{9,8},{10,11... | collective-permute-start | bytes 73736 | tf_op jit(solution)/shard_map/ppermute | solution.py:826
  346.8 5.6 %copy-start = (bf16[1,5,16,16,1024]{4,3,2,1,0:T(8,128)(2,1)S(1)}, bf16[1,5,16,16,1024]{4,3,2,1,0:T(8,128)(2,1)}, u32[]{:S(2)}) copy-start(bf16[1,5,16,16,1024]{4,3,2,1,0:T(8,128)(2,1)} %get-tuple-element.91) | copy-start | bytes 7864324
  352.4 2.7 copy-start.1
